TPU v7x, 32 devices: a whole 2x2x4 slice. The times are simulated.
32 devices in a mesh: tmpl: 4 (over y, core), seq: 2 (over x), tp: 4 (over z).
Axes of the slice: x: 2, y: 2, z: 4, core: 2. Of those that a mesh axis runs over, the one named last changes fastest.
Arguments:
- tokens: bfloat16 [3072, 5376], P(('tmpl', 'seq', 'tp')), parts along dimension 0, may hold values from -6 to 6
- lengths: int32 [8], P('tmpl'), parts along dimension 0, may hold values from 1 to 384, as said below
- input_gain: float32 [5376], replicated, may hold values from 0.1 to 1.9
- query_proj: bfloat16 [5376, 512], P(None, 'tp'), may hold values from -0.078125 to 0.078125
- key_value: bfloat16 [5376, 1024], P(None, 'tp'), may hold values from -0.078125 to 0.078125
- query_gain: float32 [128], replicated, may hold values from 0.5 to 20, as said below
- key_gain: float32 [128], replicated, may hold values from 0.5 to 6, as said below
- window_cache: bfloat16 [4096, 1024], P(('tmpl', 'seq'), 'tp'), parts along dimension 0, may hold values from -6 to 6
- output_proj: bfloat16 [512, 5376], P('tp', 'seq'), may hold values from -0.25 to 0.25
- post_gain: float32 [5376], replicated, may hold values from 0.1 to 1.9
Outputs:
- layer_out: bfloat16 [3072, 5376], P(('tmpl', 'seq', 'tp')), parts along dimension 0
There are 4 independent parts, one for each index of `tmpl`. A program takes and returns all parts, laid end to end along the dimension named above; an argument that names none is the same for every part. Nothing has to cross between parts.
Inputs may be any that keep to these rules, and one draw needn't show every extreme that they name: The template's live slab tokens fill the first lengths[s] slots of seq index s, in order of s; one entry equals 384. `query_gain`: positive entries. `key_gain`: positive entries.
All inputs are finite; a program needn't handle non-finite values.
Results may differ from a plain program's by a relative error of at most 0.018.
The roundings to bfloat16 on the way count: a program that leaves them out, or rounds other values in their place, can miss the bound.
Values may be sent and summed in bfloat16 or wider, within the bound.
A program may use at most 64 MiB of HBM per device.

v0:
```python
import functools

import jax
import jax.numpy as jnp
import numpy as np
from jax import lax
from jax.experimental import pallas as pl
from jax.experimental.pallas import tpu as pltpu
from jax.sharding import PartitionSpec as P

WIN = 1024
PREFIX = 32768
EPSILON = 1e-06
ROPE_BASE = 10000.0
QUERY_SCALE = 168.0 ** (-0.5)
MASKED = -1e30
F32 = jnp.float32
BF16 = jnp.bfloat16
MESH = pl.DeviceIdType.MESH


def chunk_of(width, limit):
    best = 128
    for c in range(128, limit + 1, 128):
        if width % c == 0:
            best = c
    return best


def flat(v):
    shape = (v.shape[0] * v.shape[1], v.shape[2])
    if v.shape[1] % 16 == 0:
        return v.reshape(shape)
    return v.astype(F32).reshape(shape).astype(v.dtype)


def kernel(
    T, S, N, S2, NC, NG,
    lengths, tokens, wq_hbm, wkv_hbm, cache_hbm, oproj_hbm,
    ig_hbm, pg_hbm, qgain, kgain, freq,
    out_ref,
    igs, pgs, igain, pgain, cos_t, sin_t, xbuf, nbuf, wq, wkv, cbuf, og, q_all, kv_all, q_snd, kv_snd, hsnd, ho, proj,
    lsem, ssem, hssem,
    r_x, r_c, r_w, r_oz, r_o, r_q, r_kv, r_kvx, r_h, r_own,
):
    t, s, z = lax.axis_index("tmpl"), lax.axis_index("seq"), lax.axis_index("tp")
    h = N // 2
    p, b = z // h, z % h
    zp = (z + h) % N
    R, D = tokens.shape
    HW = wq_hbm.shape[1]
    C = cache_hbm.shape[0]
    DE = D // (T * S2)
    OR = oproj_hbm.shape[0] // T
    DC = oproj_hbm.shape[1]
    tc = t + 1 - 2 * (t % 2)
    par = t % 2
    ys = [(t + 2 * k) % T for k in range(1, T // 2)]
    xs = [(s + k) % S for k in range(1, S)]
    sg, sb = (s // S2) * S2, s % S2
    x2 = [(sb + k) % S2 for k in range(1, S2)]
    zs = [(z + k) % N for k in range(1, N)]

    pending = []

    def queue(src, dst, rsem, dev):
        c = pltpu.make_async_remote_copy(
            src_ref=src, dst_ref=dst, send_sem=ssem.at[len(pending)], recv_sem=rsem,
            device_id=dev, device_id_type=MESH,
        )
        pending.append(c)
        return c

    def send(src, dst, rsem, dev):
        queue(src, dst, rsem, dev).start()

    def arrived(dst, rsem):
        pltpu.make_async_remote_copy(
            src_ref=dst, dst_ref=dst, send_sem=ssem.at[0], recv_sem=rsem,
            device_id={"tp": zp}, device_id_type=MESH,
        ).wait_recv()

    loc = [
        pltpu.make_async_copy(tokens, xbuf.at[b], lsem.at[0]),
        pltpu.make_async_copy(wq_hbm, wq.at[0], lsem.at[1]),
        pltpu.make_async_copy(wkv_hbm, wkv.at[0], lsem.at[2]),
        pltpu.make_async_copy(cache_hbm, cbuf.at[s], lsem.at[3]),
        pltpu.make_async_copy(
            oproj_hbm.at[pl.ds(pl.multiple_of(t * OR, OR), OR)], og.at[s, t, z], lsem.at[4]
        ),
        pltpu.make_async_copy(ig_hbm, igs, lsem.at[5]),
        pltpu.make_async_copy(pg_hbm, pgs, lsem.at[6]),
    ]
    for c in loc:
        c.start()

    barrier = pltpu.get_barrier_semaphore()
    peers = (
        [{"tp": k} for k in zs] + [{"seq": k} for k in xs]
        + [{"tmpl": k} for k in ys] + [{"tmpl": tc}]
    )
    for dev in peers:
        pl.semaphore_signal(barrier, inc=1, device_id=dev, device_id_type=MESH)
    pl.semaphore_wait(barrier, len(peers))

    DN = DE // NC

    def piece(e_t, e_s, c):
        return pl.ds(pl.multiple_of((e_t * S2 + e_s) * DE + c * DN, DN), DN)

    wset = [
        (c, a, src, buf)
        for c in range(NC)
        for a, src, buf in ((1, wkv_hbm, wkv), (0, wq_hbm, wq))
    ]
    w_first = [
        queue(
            src.at[piece(t, sb, c)], buf.at[1, piece(t, sb, c)],
            r_own.at[a, c], {"tp": zp},
        )
        for c, a, src, buf in wset
    ]
    rows_first = [
        queue(tokens, xbuf.at[b], r_x.at[b], {"tp": p * h + (b + k) % h})
        for k in range(1, h)
    ]

    out_first = [
        queue(
            oproj_hbm.at[pl.ds(pl.multiple_of(t * OR, OR), OR)], og.at[s, t, z],
            r_oz.at[z], {"tp": k},
        )
        for k in zs
    ]

    @pl.when(par == 0)
    def _():
        for c in w_first + out_first + rows_first:
            c.start()

    @pl.when(par == 1)
    def _():
        for c in rows_first + w_first + out_first:
            c.start()

    for k in xs:
        send(cache_hbm, cbuf.at[s], r_c.at[s], {"seq": k})

    GN = N // NG
    gz, zl = z // GN, z % GN
    OH = OR // 2

    def op_full(ps, pt, g):
        return og.at[ps, pt, pl.ds(g * GN, GN)]

    def op_half(ps, pt, g, f):
        return og.at[ps, pt, pl.ds(g * GN, GN), pl.ds(f * OH, OH)]

    def out_own(j):
        g = (gz + j) % NG
        for k in range(1 if j == 0 else 0, GN):
            n = g * GN + (zl + k) % GN
            arrived(og.at[s, t, n], r_oz.at[n])
        pc = op_full(s, t, g)
        for k in xs:
            send(pc, pc, r_o.at[0, s, t, g], {"seq": k})
        for k in ys:
            send(pc, pc, r_o.at[0, s, t, g], {"tmpl": k})
        send(pc, pc, r_o.at[0, s, t, g], {"tmpl": tc})

    def out_second(j):
        g = (gz + j) % NG
        for kt in ys:
            pc = op_full(s, kt, g)
            arrived(pc, r_o.at[0, s, kt, g])
            hf = op_half(s, kt, g, 0)
            for k in xs:
                send(hf, hf, r_o.at[0, s, kt, g], {"seq": k})
            send(pc, pc, r_o.at[0, s, kt, g], {"tmpl": tc})
        for ks in xs:
            pc = op_full(ks, t, g)
            arrived(pc, r_o.at[0, ks, t, g])
            hf = op_half(ks, t, g, 1)
            for k in ys:
                send(hf, hf, r_o.at[1, ks, t, g], {"tmpl": k})
            send(pc, pc, r_o.at[0, ks, t, g], {"tmpl": tc})

    def out_third(j):
        g = (gz + j) % NG
        for ks in xs:
            for kt in ys:
                for f in range(2):
                    hf = op_half(ks, kt, g, f)
                    arrived(hf, r_o.at[f, ks, kt, g])
                    send(hf, hf, r_o.at[f, ks, kt, g], {"tmpl": tc})

    def out_last(j):
        g = (gz + j) % NG
        for i in range(S):
            for m in range(T // 2):
                ks, kt = (s + i) % S, (tc + 2 * m) % T
                if i and m:
                    for f in range(2):
                        arrived(op_half(ks, kt, g, f), r_o.at[f, ks, kt, g])
                else:
                    arrived(op_full(ks, kt, g), r_o.at[0, ks, kt, g])

    loc[4].wait()
    if GN == 1:
        out_own(0)

    lens = [lengths[k] for k in range(S)]
    offs = []
    total = jnp.int32(0)
    for k in range(S):
        offs.append(total)
        total = total + lens[k]
    own_off = jnp.int32(0)
    own_len = jnp.int32(0)
    for k in range(S):
        own_off = own_off + jnp.where(s == k, offs[k], 0)
        own_len = own_len + jnp.where(s == k, lens[k], 0)

    RB = 16 if R % 16 == 0 else 8
    KC = chunk_of(D, 1024)

    def norm_rows(slot):
        def body(i, carry):
            rows = pl.ds(pl.multiple_of(i * RB, RB), RB)
            v = xbuf[slot, rows, :].astype(F32)
            inv = lax.rsqrt(jnp.sum(v * v, axis=1, keepdims=True) * (1.0 / D) + EPSILON)
            nbuf[slot, rows, :] = (v * inv * igain[...]).astype(BF16)
            return carry

        lax.fori_loop(0, R // RB, body, 0)

    def head_norm(v, gain):
        inv = lax.rsqrt(jnp.mean(v * v, axis=1, keepdims=True) + EPSILON)
        return v * inv * gain

    def project(slots, j):
        def body(i, acc):
            ks = pl.ds(pl.multiple_of(i * KC, KC), KC)
            xv = [nbuf[slot, :, ks] for slot in slots]
            xv = jnp.concatenate(xv, axis=0) if len(slots) > 1 else xv[0]
            return (
                acc[0] + jnp.dot(xv, wq[j, ks, :], preferred_element_type=F32),
                acc[1] + jnp.dot(xv, wkv[j, ks, :], preferred_element_type=F32),
            )

        M = R * len(slots)
        qr, kv = lax.fori_loop(
            0, D // KC, body, (jnp.zeros((M, HW), F32), jnp.zeros((M, 2 * HW), F32))
        )
        out = []
        for i, slot in enumerate(slots):
            co, si = cos_t[slot], sin_t[slot]
            rows = slice(i * R, (i + 1) * R)

            def rope(u):
                return u * co + pltpu.roll(u, HW // 2, 1) * si

            q = (rope(head_norm(qr[rows], qgain[...])) * QUERY_SCALE).astype(BF16)
            k = rope(head_norm(kv[rows, :HW], kgain[...])).astype(BF16)
            out.append((q, jnp.concatenate([k, kv[rows, HW:].astype(BF16)], axis=1)))
        return out

    def own_head(slot):
        q, kv = project([slot], 0)[0]
        n = p * h + slot
        q_all[n] = q
        kv_all[s, n] = kv
        for k in xs:
            send(kv_all.at[s, n], kv_all.at[s, n], r_kvx.at[s, n], {"seq": k})

    def other_head(slot, q, kv):
        n = p * h + slot
        q_snd[slot] = q
        kv_snd[slot] = kv
        send(kv_snd.at[slot], kv_all.at[s, n], r_kv.at[n], {"tp": zp})
        send(q_snd.at[slot], q_all.at[n], r_q.at[n], {"tp": zp})

    loc[5].wait()
    loc[6].wait()
    for k in range(D // 128):
        igain[0:1, k * 128 : (k + 1) * 128] = igs[k : k + 1, :]
        pgain[0:1, k * 128 : (k + 1) * 128] = pgs[k : k + 1, :]
    lane = lax.broadcasted_iota(jnp.int32, (R, HW), 1)
    for k in range(h):
        row = lax.broadcasted_iota(jnp.int32, (R, HW), 0)
        angle = (PREFIX + own_off + (p * h + k) * R + row).astype(F32) * freq[...]
        cos_t[k] = jnp.cos(angle)
        sine = jnp.sin(angle)
        sin_t[k] = jnp.where(lane < HW // 2, -sine, sine)
    loc[0].wait()
    norm_rows(b)
    loc[1].wait()
    loc[2].wait()
    own_head(b)

    def w_own(c, a, src, buf):
        pc = buf.at[1, piece(t, sb, c)]
        arrived(pc, r_own.at[a, c])
        for k in x2:
            send(pc, pc, r_w.at[a, t, sb, c], {"seq": sg + k})
        for k in ys:
            send(pc, pc, r_w.at[a, t, sb, c], {"tmpl": k})
        send(pc, pc, r_w.at[a, t, sb, c], {"tmpl": tc})

    def w_x(c, a, src, buf):
        for k2 in x2:
            pc = buf.at[1, piece(t, k2, c)]
            arrived(pc, r_w.at[a, t, k2, c])
            for k in ys:
                send(pc, pc, r_w.at[a, t, k2, c], {"tmpl": k})
            send(pc, pc, r_w.at[a, t, k2, c], {"tmpl": tc})

    def w_y(c, a, src, buf):
        for k in ys:
            for k2 in range(S2):
                ks = (sb + k2) % S2
                pc = buf.at[1, piece(k, ks, c)]
                arrived(pc, r_w.at[a, k, ks, c])
                send(pc, pc, r_w.at[a, k, ks, c], {"tmpl": tc})

    for i in range(NC + 1):
        if i < NC:
            for w in wset[2 * i : 2 * i + 2]:
                w_own(*w)
        if i == 0 and GN == 1:
            out_second(0)
        if i > 0:
            for w in wset[2 * i - 2 : 2 * i]:
                w_x(*w)
    for j in range(1 if GN == 1 else 0, NG):
        out_own(j)

    for w in wset:
        w_y(*w)

    for k in range(1, h):
        slot = (b + k) % h
        arrived(xbuf.at[slot], r_x.at[slot])
        norm_rows(slot)
        own_head(slot)
    for c, a, src, buf in wset:
        for k in range(T // 2):
            kt = (1 - par) + 2 * k
            for ks in range(S2):
                arrived(buf.at[1, piece(kt, ks, c)], r_w.at[a, kt, ks, c])
    if R % 16 == 0:
        done = project(list(range(h)), 1)
    else:
        done = [project([k], 1)[0] for k in range(h)]
    for k in range(h):
        other_head(k, *done[k])

    op = 1 - p
    for i in range(h):
        n = op * h + i
        arrived(kv_all.at[s, n], r_kv.at[n])
        for k in xs:
            send(kv_all.at[s, n], kv_all.at[s, n], r_kvx.at[s, n], {"seq": k})
    for i in range(h):
        n = op * h + i
        arrived(q_all.at[n], r_q.at[n])
    for j in range(1 if GN == 1 else 0, NG):
        out_second(j)
    loc[3].wait()
    for k in xs:
        arrived(cbuf.at[k], r_c.at[k])
        for n in range(N):
            arrived(kv_all.at[k, n], r_kvx.at[k, n])

    def attend(d, carry):
        n = lax.rem(z + d, N)
        q = q_all[n]
        slot_c = n * R + lax.broadcasted_iota(jnp.int32, (R, 1), 0)
        pos = PREFIX + own_off + slot_c
        scores, allow, values = [], [], []
        for k in range(S):
            cb = cbuf[k]
            sc = lax.dot_general(
                q, cb[:, :HW], (((1,), (1,)), ((), ())), preferred_element_type=F32
            )
            kp = PREFIX - WIN + k * C + lax.broadcasted_iota(jnp.int32, (1, C), 1)
            ok = (kp <= pos) & (kp > pos - WIN)
            scores.append(jnp.where(ok, sc, MASKED))
            allow.append(ok)
            values.append(cb[:, HW:])
            kv = flat(kv_all[k])
            sc = lax.dot_general(
                q, kv[:, :HW], (((1,), (1,)), ((), ())), preferred_element_type=F32
            )
            j = lax.broadcasted_iota(jnp.int32, (1, N * R), 1)
            kp = PREFIX + offs[k] + j
            ok = (kp <= pos) & (kp > pos - WIN) & (j < lens[k])
            scores.append(jnp.where(ok, sc, MASKED))
            allow.append(ok)
            values.append(kv[:, HW:])
        top = functools.reduce(
            jnp.maximum, [jnp.max(v, axis=1, keepdims=True) for v in scores]
        )
        row_sum = jnp.zeros((R, 1), F32)
        acc = jnp.zeros((R, HW), F32)
        for sc, ok, vv in zip(scores, allow, values):
            w = jnp.where(ok, jnp.exp(sc - top), 0.0)
            row_sum = row_sum + jnp.sum(w, axis=1, keepdims=True)
            acc = acc + jnp.dot(w.astype(BF16), vv, preferred_element_type=F32)
        live = slot_c < own_len
        res = acc / jnp.where(live, row_sum, 1.0)
        hsnd[n] = jnp.where(live, res, 0.0).astype(BF16)

        @pl.when(d < N)
        def _():
            pltpu.make_async_remote_copy(
                src_ref=hsnd.at[n], dst_ref=ho.at[z], send_sem=hssem.at[n],
                recv_sem=r_h.at[z], device_id={"tp": n}, device_id_type=MESH,
            ).start()

        return carry

    lax.fori_loop(1, N + 1, attend, 0)
    ho[z] = hsnd[z]

    for j in range(NG):
        out_third(j)
    for j in range(NG):
        out_last(j)
    for k in zs:
        arrived(ho.at[k], r_h.at[k])

    CC = chunk_of(DC, 1024)

    for k in range(S):
        def cols(i, carry):
            cs = pl.ds(pl.multiple_of(i * CC, CC), CC)
            acc = jnp.zeros((R, CC), F32)
            for g in range(N):
                w = jnp.concatenate([og[k, kt, g, :, cs] for kt in range(T)], axis=0)
                acc = acc + jnp.dot(ho[g], w, preferred_element_type=F32).astype(BF16).astype(F32)
            proj[:, pl.ds(pl.multiple_of(k * DC + i * CC, 128), CC)] = acc
            return carry

        lax.fori_loop(0, DC // CC, cols, 0)

    def finish(i, carry):
        rows = pl.ds(pl.multiple_of(i * RB, RB), RB)
        v = proj[rows, :]
        inv = lax.rsqrt(jnp.sum(v * v, axis=1, keepdims=True) * (1.0 / D) + EPSILON)
        out_ref[rows, :] = (xbuf[b, rows, :].astype(F32) + v * inv * pgain[...]).astype(BF16)
        return carry

    lax.fori_loop(0, R // RB, finish, 0)

    for c in pending:
        c.wait_send()
    for k in zs:
        pltpu.make_async_remote_copy(
            src_ref=hsnd.at[k], dst_ref=ho.at[z], send_sem=hssem.at[k],
            recv_sem=r_h.at[z], device_id={"tp": k}, device_id_type=MESH,
        ).wait_send()


def shards(
    T, S, N,
    tokens, lengths, input_gain, query_proj, key_value, query_gain, key_gain,
    window_cache, output_proj, post_gain,
):
    R, D = tokens.shape
    HW = query_proj.shape[1]
    C = window_cache.shape[0]
    h = N // 2
    S2 = max(d for d in range(1, S + 1) if S % d == 0 and D % (16 * T * d) == 0)
    NC = max(d for d in (1, 2, 3, 6) if D // (T * S2) % (16 * d) == 0)
    NG = max(d for d in (1, 2, 4) if N % d == 0)
    inv = np.power(ROPE_BASE, -2.0 * np.arange(HW // 2) / HW)
    freq = np.concatenate([inv, inv])[None, :].astype(np.float32)
    OR, DC = output_proj.shape[0] // T, output_proj.shape[1]
    Y = T // 2 - 1
    w_sends = 2 * NC * (1 + (S2 + Y) + (S2 - 1) * (Y + 1) + Y * S2)
    o_sends = (N - 1) + NG * ((S + Y) + Y * S + (S - 1) * (Y + 1) + 2 * (S - 1) * Y)
    sends = w_sends + o_sends + (h - 1) + (S - 1) + N * (S - 1) + 2 * h
    held = 3 * h * R * D * 2 + 6 * D * HW * 2 + 2 * S * C * HW * 2 + S * T * N * OR * DC * 2
    held += (6 + 2 * S) * N * R * HW * 2 + R * D * 4 + R * D * 2
    vm = pl.BlockSpec(memory_space=pltpu.VMEM)
    hb = pl.BlockSpec(memory_space=pltpu.HBM)
    dma = pltpu.SemaphoreType.DMA
    return pl.pallas_call(
        functools.partial(kernel, T, S, N, S2, NC, NG),
        out_shape=jax.ShapeDtypeStruct((R, D), BF16),
        in_specs=[pl.BlockSpec(memory_space=pltpu.SMEM), hb, hb, hb, hb, hb]
        + [hb, hb, vm, vm, vm],
        out_specs=vm,
        scratch_shapes=[
            pltpu.VMEM((D // 128, 128), F32),
            pltpu.VMEM((D // 128, 128), F32),
            pltpu.VMEM((1, D), F32),
            pltpu.VMEM((1, D), F32),
            pltpu.VMEM((h, R, HW), F32),
            pltpu.VMEM((h, R, HW), F32),
            pltpu.VMEM((h, R, D), BF16),
            pltpu.VMEM((h, R, D), BF16),
            pltpu.VMEM((2, D, HW), BF16),
            pltpu.VMEM((2, D, 2 * HW), BF16),
            pltpu.VMEM((S, C, 2 * HW), BF16),
            pltpu.VMEM((S, T, N, OR, DC), BF16),
            pltpu.VMEM((N, R, HW), BF16),
            pltpu.VMEM((S, N, R, 2 * HW), BF16),
            pltpu.VMEM((h, R, HW), BF16),
            pltpu.VMEM((h, R, 2 * HW), BF16),
            pltpu.VMEM((N, R, HW), BF16),
            pltpu.VMEM((N, R, HW), BF16),
            pltpu.VMEM((R, D), F32),
            dma((7,)), dma((sends,)), dma((N,)),
            dma((h,)), dma((S,)), dma((2, T, S2, NC)), dma((N,)), dma((2, S, T, NG)),
            dma((N,)), dma((N,)), dma((S, N)), dma((N,)), dma((2, NC)),
        ],
        compiler_params=pltpu.CompilerParams(
            collective_id=0, has_side_effects=True, vmem_limit_bytes=67043328 - 2 * R * D * 2
        ),
    )(
        lengths, tokens, query_proj, key_value, window_cache, output_proj,
        input_gain.reshape(D // 128, 128), post_gain.reshape(D // 128, 128),
        query_gain[None, :], key_gain[None, :], jnp.asarray(freq),
    )


def solution(mesh):
    T, S, N = mesh.shape["tmpl"], mesh.shape["seq"], mesh.shape["tp"]
    return jax.shard_map(
        functools.partial(shards, T, S, N),
        mesh=mesh,
        in_specs=(
            P(("tmpl", "seq", "tp"), None),
            P("tmpl"),
            P(),
            P(None, "tp"),
            P(None, "tp"),
            P(),
            P(),
            P(("tmpl", "seq"), "tp"),
            P("tp", "seq"),
            P(),
        ),
        out_specs=P(("tmpl", "seq", "tp"), None),
        check_vma=False,
    )
```

profile of v0, /device:TPU:0, one launch (start us, length us, event | category | flops | bytes accessed | tf_op | source)
XLA Modules:
  0.0 82.0 jit_solution(628191981790466497)
XLA Ops:
  0.0 79.8 %shard_map.109 = bf16[96,5376]{1,0:T(8,128)(2,1)} custom-call(s32[2]{0:T(128)} %lengths.1, bf16[96,5376]{1,0:T(8,128)(2,1)} %tokens.1, bf16[5376,128]{1,0:T(8,128)(2,1)} %wq_hbm.1, bf16[5376,256]{1,0:T(8,128)(2,1)} %wkv_hbm.1, bf16[512,256]{1,0:T(8,128)(2,1)} %cache_hbm.1, bf16[128,2688]{1,0:T(8,128)(2,1)} %oproj_hbm.1, f32[42,128]{1,0:T(8,128)} %bitcast.4, ...), custom_call_target="tpu_custom_call" | custom-call | tf_op jit(solution)/shard_map/pallas_call | solution.py:489
  79.8 2.2 %copy.13 = bf16[96,5376]{1,0:T(8,128)(2,1)} copy(bf16[96,5376]{1,0:T(8,128)(2,1)} %shard_map.109) | data formatting | bytes 2064384
where the time goes:
time: 83.2 us; the launch traced here: 82 us
  Pallas kernels  79.8 us (96%)
  local copies, waits for them, and re-layouts  2.25 us (3%)
    pallas_call x1, Pallas kernels, shards(): pl.pallas_call(functools.partial(kernel, T, S, N, S2, NC, NG), out_shape=...  79.8 us
    unnamed x1, local copies, waits for them, and re-layouts  2.25 us

commit v1 on v0

v1 whole, which is shorter than its diff:
```python
import functools

import jax
import jax.numpy as jnp
import numpy as np
from jax import lax
from jax.experimental import pallas as pl
from jax.experimental.pallas import tpu as pltpu
from jax.sharding import PartitionSpec as P

WIN = 1024
PREFIX = 32768
EPSILON = 1e-06
ROPE_BASE = 10000.0
QUERY_SCALE = 168.0 ** (-0.5)
MASKED = -1e30
F32 = jnp.float32
BF16 = jnp.bfloat16
MESH = pl.DeviceIdType.MESH


def chunk_of(width, limit):
    best = 128
    for c in range(128, limit + 1, 128):
        if width % c == 0:
            best = c
    return best


def flat(v):
    shape = (v.shape[0] * v.shape[1], v.shape[2])
    if v.shape[1] % 16 == 0:
        return v.reshape(shape)
    return v.astype(F32).reshape(shape).astype(v.dtype)


def kernel(
    T, S, N, S2, NC, RC,
    lengths, tokens, wq_hbm, wkv_hbm, cache_hbm, oproj_hbm,
    ig_hbm, pg_hbm, qgain, kgain, freq,
    out_ref,
    igs, pgs, igain, pgain, cos_t, sin_t, xbuf, nbuf, w, cbuf, og, q_all, kv_all, q_snd, kv_snd, hsnd, ho, proj,
    lsem, s_w, s_x, s_c, s_o, s_oz, s_kvx, s_kv, s_q, s_h,
    r_x, r_c, r_own, r_w, r_o, r_q, r_kv, r_kvx, r_h,
):
    t, s, z = lax.axis_index("tmpl"), lax.axis_index("seq"), lax.axis_index("tp")
    h = N // 2
    p, b = z // h, z % h
    op = 1 - p
    zp = (z + h) % N
    R, D = tokens.shape
    HW = wq_hbm.shape[1]
    C = cache_hbm.shape[0]
    DE = D // (T * S2)
    DN = DE // NC
    RR = R // RC
    OR = oproj_hbm.shape[0] // T
    DC = oproj_hbm.shape[1]
    tc = t + 1 - 2 * (t % 2)
    par = t % 2
    ys = [(t + 2 * k) % T for k in range(1, T // 2)]
    same = [t] + ys
    cross = [(tc + 2 * k) % T for k in range(T // 2)]
    xs = [(s + k) % S for k in range(1, S)]
    sg, sb = (s // S2) * S2, s % S2
    x2 = [(sb + k) % S2 for k in range(1, S2)]
    zs = [(z + k) % N for k in range(1, N)]

    def copy(src, dst, ssem, rsem, dev):
        return pltpu.make_async_remote_copy(
            src_ref=src, dst_ref=dst, send_sem=ssem, recv_sem=rsem,
            device_id=dev, device_id_type=MESH,
        )

    def send(src, dst, ssem, rsem, dev):
        copy(src, dst, ssem, rsem, dev).start()

    def arrived(dst, rsem):
        copy(dst, dst, s_q, rsem, {"tp": zp}).wait_recv()

    def left(src, ssem):
        copy(src, src, ssem, r_q, {"tp": zp}).wait_send()

    loc = [
        pltpu.make_async_copy(tokens, xbuf.at[b], lsem.at[0]),
        pltpu.make_async_copy(wq_hbm, w.at[0, :, pl.ds(0, HW)], lsem.at[1]),
        pltpu.make_async_copy(wkv_hbm, w.at[0, :, pl.ds(HW, 2 * HW)], lsem.at[2]),
        pltpu.make_async_copy(ig_hbm, igs, lsem.at[3]),
        pltpu.make_async_copy(pg_hbm, pgs, lsem.at[4]),
        pltpu.make_async_copy(cache_hbm, cbuf.at[s], lsem.at[5]),
    ]

    def slab(ks, kt, n):
        return (ks * T + kt) * N + n

    for k in range(T):
        loc.append(
            pltpu.make_async_copy(
                oproj_hbm.at[pl.ds(k * OR, OR)], og.at[slab(s, k, z)], lsem.at[6 + k]
            )
        )
    for c in loc:
        c.start()

    barrier = pltpu.get_barrier_semaphore()
    peers = (
        [{"tp": k} for k in zs] + [{"seq": k} for k in xs]
        + [{"tmpl": k} for k in ys] + [{"tmpl": tc}]
    )
    for dev in peers:
        pl.semaphore_signal(barrier, inc=1, device_id=dev, device_id_type=MESH)
    pl.semaphore_wait(barrier, len(peers))

    def piece(e_t, e_s, c):
        return pl.ds(pl.multiple_of((e_t * S2 + e_s) * DE + c * DN, DN), DN)

    loc[1].wait()
    loc[2].wait()

    def send_w():
        for c in range(NC):
            pc = piece(t, sb, c)
            send(w.at[0, pc], w.at[1, pc], s_w, r_own.at[c], {"tp": zp})

    def send_rows(c):
        rows = pl.ds(c * RR, RR)
        for k in range(1, h):
            send(tokens.at[rows], xbuf.at[b, rows], s_x, r_x.at[b, c], {"tp": p * h + (b + k) % h})

    @pl.when(par == 0)
    def _():
        send_w()
        for c in range(RC):
            send_rows(c)

    @pl.when(par == 1)
    def _():
        send_rows(0)
        send_w()
        for c in range(1, RC):
            send_rows(c)

    for k in xs:
        send(cache_hbm, cbuf.at[s], s_c, r_c.at[s], {"seq": k})

    lens = [lengths[k] for k in range(S)]
    offs = []
    total = jnp.int32(0)
    for k in range(S):
        offs.append(total)
        total = total + lens[k]
    own_off = jnp.int32(0)
    own_len = jnp.int32(0)
    for k in range(S):
        own_off = own_off + jnp.where(s == k, offs[k], 0)
        own_len = own_len + jnp.where(s == k, lens[k], 0)

    RB = 16 if RR % 16 == 0 else 8
    KC = chunk_of(D, 1024)

    def norm_rows(slot, first, count):
        def body(i, carry):
            rows = pl.ds(pl.multiple_of(first + i * RB, RB), RB)
            v = xbuf[slot, rows, :].astype(F32)
            inv = lax.rsqrt(jnp.sum(v * v, axis=1, keepdims=True) * (1.0 / D) + EPSILON)
            nbuf[slot, rows, :] = (v * inv * igain[...]).astype(BF16)
            return carry

        lax.fori_loop(0, count // RB, body, 0)

    def head_norm(v, gain):
        inv = lax.rsqrt(jnp.mean(v * v, axis=1, keepdims=True) + EPSILON)
        return v * inv * gain

    def project(slot, j):
        def body(i, acc):
            ks = pl.ds(pl.multiple_of(i * KC, KC), KC)
            return acc + jnp.dot(nbuf[slot, :, ks], w[j, ks, :], preferred_element_type=F32)

        v = lax.fori_loop(0, D // KC, body, jnp.zeros((R, 3 * HW), F32))
        co, si = cos_t[slot], sin_t[slot]

        def rope(u):
            return u * co + pltpu.roll(u, HW // 2, 1) * si

        q = (rope(head_norm(v[:, :HW], qgain[...])) * QUERY_SCALE).astype(BF16)
        k = rope(head_norm(v[:, HW : 2 * HW], kgain[...])).astype(BF16)
        return q, jnp.concatenate([k, v[:, 2 * HW :].astype(BF16)], axis=1)

    def share(n):
        for k in xs:
            send(kv_all.at[s, n], kv_all.at[s, n], s_kvx, r_kvx.at[s], {"seq": k})

    def own_head(slot):
        q, kv = project(slot, 0)
        n = p * h + slot
        q_all[n] = q
        kv_all[s, n] = kv
        share(n)

    def other_head(slot):
        q, kv = project(slot, 1)
        n = p * h + slot
        q_snd[slot] = q
        kv_snd[slot] = kv
        send(kv_snd.at[slot], kv_all.at[s, n], s_kv, r_kv, {"tp": zp})
        send(q_snd.at[slot], q_all.at[n], s_q, r_q, {"tp": zp})

    loc[3].wait()
    loc[4].wait()
    for k in range(D // 128):
        igain[0:1, k * 128 : (k + 1) * 128] = igs[k : k + 1, :]
        pgain[0:1, k * 128 : (k + 1) * 128] = pgs[k : k + 1, :]
    lane = lax.broadcasted_iota(jnp.int32, (R, HW), 1)
    for k in range(h):
        row = lax.broadcasted_iota(jnp.int32, (R, HW), 0)
        angle = (PREFIX + own_off + (p * h + k) * R + row).astype(F32) * freq[...]
        cos_t[k] = jnp.cos(angle)
        sine = jnp.sin(angle)
        sin_t[k] = jnp.where(lane < HW // 2, -sine, sine)
    loc[0].wait()
    norm_rows(b, 0, R)
    own_head(b)
    for k in range(T):
        loc[6 + k].wait()

    def o_copy(idx, dev, ssem=None):
        send(og.at[idx], og.at[idx], s_o if ssem is None else ssem, r_o.at[idx], dev)

    def z_right(n):
        @pl.when(z < N - 1)
        def _():
            o_copy(slab(s, t, n), {"tp": jnp.minimum(z + 1, N - 1)}, s_oz.at[n])

    def z_left(n):
        @pl.when(z > 0)
        def _():
            o_copy(slab(s, t, n), {"tp": jnp.maximum(z - 1, 0)}, s_oz.at[N + n])

    def o_arrive(d):
        @pl.when(z + d < N)
        def _():
            n = z + d
            arrived(og.at[slab(s, t, n)], r_o.at[slab(s, t, n)])
            z_left(n)
            o_plane(n)

        @pl.when(z - d >= 0)
        def _():
            n = z - d
            arrived(og.at[slab(s, t, n)], r_o.at[slab(s, t, n)])
            z_right(n)
            o_plane(n)

    def o_plane(n):
        i = slab(s, t, n)
        for k in xs:
            o_copy(i, {"seq": k})
        for k in ys:
            o_copy(i, {"tmpl": k})
        o_copy(i, {"tmpl": tc})

    def each(d, fn):
        @pl.when(z + d < N)
        def _():
            fn(z + d)

        @pl.when(z - d >= 0)
        def _():
            fn(z - d)

    def o_x(n):
        for ks in xs:
            i = slab(ks, t, n)
            arrived(og.at[i], r_o.at[i])
            for k in ys:
                o_copy(i, {"tmpl": k})
            o_copy(i, {"tmpl": tc})

    def o_y(n):
        for kt in ys:
            for ks in [s] + xs:
                i = slab(ks, kt, n)
                arrived(og.at[i], r_o.at[i])
                o_copy(i, {"tmpl": tc})

    def o_last(n):
        for kt in cross:
            for ks in [s] + xs:
                i = slab(ks, kt, n)
                arrived(og.at[i], r_o.at[i])

    def own_x():
        for kt in same:
            for k in xs:
                o_copy(slab(s, kt, z), {"seq": k})

    def own_c():
        for ks in xs:
            for kt in same:
                i = slab(ks, kt, z)
                arrived(og.at[i], r_o.at[i])
                o_copy(i, {"tmpl": tc})

    def own_last():
        for ks in xs:
            for kt in cross:
                i = slab(ks, kt, z)
                arrived(og.at[i], r_o.at[i])

    z_right(z)
    z_left(z)

    def w_own(c):
        pc = piece(t, sb, c)
        arrived(w.at[1, pc], r_own.at[c])
        for k in x2:
            send(w.at[1, pc], w.at[1, pc], s_w, r_w.at[t, sb, c], {"seq": sg + k})
        for k in ys:
            send(w.at[1, pc], w.at[1, pc], s_w, r_w.at[t, sb, c], {"tmpl": k})
        send(w.at[1, pc], w.at[1, pc], s_w, r_w.at[t, sb, c], {"tmpl": tc})

    def w_x(c):
        for k2 in x2:
            pc = piece(t, k2, c)
            arrived(w.at[1, pc], r_w.at[t, k2, c])
            for k in ys:
                send(w.at[1, pc], w.at[1, pc], s_w, r_w.at[t, k2, c], {"tmpl": k})
            send(w.at[1, pc], w.at[1, pc], s_w, r_w.at[t, k2, c], {"tmpl": tc})

    def w_y(c):
        for k in ys:
            for ks in range(S2):
                pc = piece(k, ks, c)
                arrived(w.at[1, pc], r_w.at[k, ks, c])
                send(w.at[1, pc], w.at[1, pc], s_w, r_w.at[k, ks, c], {"tmpl": tc})

    for i in range(NC + 1):
        if i < NC:
            w_own(i)
        if i > 0:
            w_x(i - 1)
    own_x()
    for c in range(NC):
        w_y(c)
    for c in range(NC):
        for kt in cross:
            for ks in range(S2):
                arrived(w.at[1, piece(kt, ks, c)], r_w.at[kt, ks, c])
    other_head(b)
    for k in range(1, h):
        slot = (b + k) % h
        for c in range(RC):
            rows = pl.ds(c * RR, RR)
            arrived(xbuf.at[slot, rows], r_x.at[slot, c])
            norm_rows(slot, c * RR, RR)
        other_head(slot)
    for k in range(1, h):
        own_head((b + k) % h)

    own_c()
    o_arrive(1)
    arrived(kv_all.at[s, pl.ds(op * h, h)], r_kv)
    for i in range(h):
        share(op * h + i)
    arrived(q_all.at[pl.ds(op * h, h)], r_q)
    each(1, o_x)
    loc[5].wait()
    for k in xs:
        arrived(cbuf.at[k], r_c.at[k])
        arrived(kv_all.at[k], r_kvx.at[k])

    def attend(d, carry):
        n = lax.rem(z + d, N)
        q = q_all[n]
        slot_c = n * R + lax.broadcasted_iota(jnp.int32, (R, 1), 0)
        pos = PREFIX + own_off + slot_c
        scores, allow, values = [], [], []
        for k in range(S):
            cb = cbuf[k]
            sc = lax.dot_general(
                q, cb[:, :HW], (((1,), (1,)), ((), ())), preferred_element_type=F32
            )
            kp = PREFIX - WIN + k * C + lax.broadcasted_iota(jnp.int32, (1, C), 1)
            ok = (kp <= pos) & (kp > pos - WIN)
            scores.append(jnp.where(ok, sc, MASKED))
            allow.append(ok)
            values.append(cb[:, HW:])
            kv = flat(kv_all[k])
            sc = lax.dot_general(
                q, kv[:, :HW], (((1,), (1,)), ((), ())), preferred_element_type=F32
            )
            j = lax.broadcasted_iota(jnp.int32, (1, N * R), 1)
            kp = PREFIX + offs[k] + j
            ok = (kp <= pos) & (kp > pos - WIN) & (j < lens[k])
            scores.append(jnp.where(ok, sc, MASKED))
            allow.append(ok)
            values.append(kv[:, HW:])
        top = functools.reduce(
            jnp.maximum, [jnp.max(v, axis=1, keepdims=True) for v in scores]
        )
        row_sum = jnp.zeros((R, 1), F32)
        acc = jnp.zeros((R, HW), F32)
        for sc, ok, vv in zip(scores, allow, values):
            wt = jnp.where(ok, jnp.exp(sc - top), 0.0)
            row_sum = row_sum + jnp.sum(wt, axis=1, keepdims=True)
            acc = acc + jnp.dot(wt.astype(BF16), vv, preferred_element_type=F32)
        live = slot_c < own_len
        res = acc / jnp.where(live, row_sum, 1.0)
        hsnd[n] = jnp.where(live, res, 0.0).astype(BF16)

        @pl.when(d < N)
        def _():
            send(hsnd.at[n], ho.at[z], s_h, r_h, {"tp": n})

        return carry

    lax.fori_loop(1, N + 1, attend, 0)
    ho[z] = hsnd[z]

    for d in range(2, N):
        o_arrive(d)
        each(d - 1, o_y)
        each(d, o_x)
    each(N - 1, o_y)
    own_last()
    for d in range(1, N):
        each(d, o_last)
    arrived(ho.at[pl.ds(0, N - 1)], r_h)

    CC = chunk_of(DC, 1024)

    for k in range(S):
        def cols(i, carry):
            cs = pl.ds(pl.multiple_of(i * CC, CC), CC)
            acc = jnp.zeros((R, CC), F32)
            for g in range(N):
                wt = jnp.concatenate([og[slab(k, kt, g), :, cs] for kt in range(T)], axis=0)
                acc = acc + jnp.dot(ho[g], wt, preferred_element_type=F32).astype(BF16).astype(F32)
            proj[:, pl.ds(pl.multiple_of(k * DC + i * CC, 128), CC)] = acc
            return carry

        lax.fori_loop(0, DC // CC, cols, 0)

    RF = 16 if R % 16 == 0 else 8

    def finish(i, carry):
        rows = pl.ds(pl.multiple_of(i * RF, RF), RF)
        v = proj[rows, :]
        inv = lax.rsqrt(jnp.sum(v * v, axis=1, keepdims=True) * (1.0 / D) + EPSILON)
        out_ref[rows, :] = (xbuf[b, rows, :].astype(F32) + v * inv * pgain[...]).astype(BF16)
        return carry

    lax.fori_loop(0, R // RF, finish, 0)

    left(w.at[1], s_w)
    left(xbuf.at[pl.ds(0, h - 1)], s_x)
    left(cbuf.at[pl.ds(0, S - 1)], s_c)
    left(kv_all.at[pl.ds(0, S - 1)], s_kvx)
    left(kv_snd, s_kv)
    left(q_snd, s_q)
    left(hsnd.at[pl.ds(0, N - 1)], s_h)
    X, Y = S - 1, T // 2 - 1
    count = (N - 1) * (X + Y + 1 + X * (Y + 1) + Y * S) + (Y + 1) * X * 2
    while count > 0:
        part = min(count, S * T * N)
        left(og.at[pl.ds(0, part)], s_o)
        count -= part
    for n in range(N):
        @pl.when((n <= z) & (z < N - 1))
        def _():
            left(og.at[0], s_oz.at[n])

        @pl.when((n >= z) & (z > 0))
        def _():
            left(og.at[0], s_oz.at[N + n])


def shards(
    T, S, N,
    tokens, lengths, input_gain, query_proj, key_value, query_gain, key_gain,
    window_cache, output_proj, post_gain,
):
    R, D = tokens.shape
    HW = query_proj.shape[1]
    C = window_cache.shape[0]
    h = N // 2
    S2 = max(d for d in range(1, S + 1) if S % d == 0 and D % (16 * T * d) == 0)
    NC = max(d for d in (1, 2, 3) if D // (T * S2) % (16 * d) == 0)
    RC = 3 if R % 48 == 0 else 1
    inv = np.power(ROPE_BASE, -2.0 * np.arange(HW // 2) / HW)
    freq = np.concatenate([inv, inv])[None, :].astype(np.float32)
    OR, DC = output_proj.shape[0] // T, output_proj.shape[1]
    vm = pl.BlockSpec(memory_space=pltpu.VMEM)
    hb = pl.BlockSpec(memory_space=pltpu.HBM)
    dma = pltpu.SemaphoreType.DMA
    return pl.pallas_call(
        functools.partial(kernel, T, S, N, S2, NC, RC),
        out_shape=jax.ShapeDtypeStruct((R, D), BF16),
        in_specs=[pl.BlockSpec(memory_space=pltpu.SMEM), hb, hb, hb, hb, hb]
        + [hb, hb, vm, vm, vm],
        out_specs=vm,
        scratch_shapes=[
            pltpu.VMEM((D // 128, 128), F32),
            pltpu.VMEM((D // 128, 128), F32),
            pltpu.VMEM((1, D), F32),
            pltpu.VMEM((1, D), F32),
            pltpu.VMEM((h, R, HW), F32),
            pltpu.VMEM((h, R, HW), F32),
            pltpu.VMEM((h, R, D), BF16),
            pltpu.VMEM((h, R, D), BF16),
            pltpu.VMEM((2, D, 3 * HW), BF16),
            pltpu.VMEM((S, C, 2 * HW), BF16),
            pltpu.VMEM((S * T * N, OR, DC), BF16),
            pltpu.VMEM((N, R, HW), BF16),
            pltpu.VMEM((S, N, R, 2 * HW), BF16),
            pltpu.VMEM((h, R, HW), BF16),
            pltpu.VMEM((h, R, 2 * HW), BF16),
            pltpu.VMEM((N, R, HW), BF16),
            pltpu.VMEM((N, R, HW), BF16),
            pltpu.VMEM((R, D), F32),
            dma((6 + T,)), dma, dma, dma, dma, dma((2 * N,)), dma, dma, dma, dma,
            dma((h, RC)), dma((S,)), dma((NC,)), dma((T, S2, NC)), dma((S * T * N,)),
            dma, dma, dma((S,)), dma,
        ],
        compiler_params=pltpu.CompilerParams(
            collective_id=0, has_side_effects=True, vmem_limit_bytes=67043328 - 2 * R * D * 2
        ),
    )(
        lengths, tokens, query_proj, key_value, window_cache, output_proj,
        input_gain.reshape(D // 128, 128), post_gain.reshape(D // 128, 128),
        query_gain[None, :], key_gain[None, :], jnp.asarray(freq),
    )


def solution(mesh):
    T, S, N = mesh.shape["tmpl"], mesh.shape["seq"], mesh.shape["tp"]
    return jax.shard_map(
        functools.partial(shards, T, S, N),
        mesh=mesh,
        in_specs=(
            P(("tmpl", "seq", "tp"), None),
            P("tmpl"),
            P(),
            P(None, "tp"),
            P(None, "tp"),
            P(),
            P(),
            P(("tmpl", "seq"), "tp"),
            P("tp", "seq"),
            P(),
        ),
        out_specs=P(("tmpl", "seq", "tp"), None),
        check_vma=False,
    )
```

time: 83.2 us -> 90.3 us (1.085)
  Pallas kernels: 79.8 us -> 87.3 us
    pallas_call x1, Pallas kernels: 79.8 us -> 87.3 us  [shards(): pl.pallas_call(functools.partial(kernel, T, S, N, S2, NC, RC), out_shape=...]
where the time goes in v1:
time: 90.3 us; the launch traced here: 89.5 us
  Pallas kernels  87.3 us (97%)
  local copies, waits for them, and re-layouts  2.25 us (2%)
    pallas_call x1, Pallas kernels, shards(): pl.pallas_call(functools.partial(kernel, T, S, N, S2, NC, RC), out_shape=...  87.3 us
    unnamed x1, local copies, waits for them, and re-layouts  2.25 us

profile of v1, /device:TPU:0, one launch (start us, length us, event | category | flops | bytes accessed | tf_op | source)
XLA Modules:
  0.0 89.5 jit_solution(11426905232445400961)
XLA Ops:
  0.0 87.3 %shard_map.109 = bf16[96,5376]{1,0:T(8,128)(2,1)} custom-call(s32[2]{0:T(128)} %lengths.1, bf16[96,5376]{1,0:T(8,128)(2,1)} %tokens.1, bf16[5376,128]{1,0:T(8,128)(2,1)} %wq_hbm.1, bf16[5376,256]{1,0:T(8,128)(2,1)} %wkv_hbm.1, bf16[512,256]{1,0:T(8,128)(2,1)} %cache_hbm.1, bf16[128,2688]{1,0:T(8,128)(2,1)} %oproj_hbm.1, f32[42,128]{1,0:T(8,128)} %bitcast.4, ...), custom_call_target="tpu_custom_call" | custom-call | tf_op jit(solution)/shard_map/pallas_call | solution.py:497
  87.3 2.2 %copy.13 = bf16[96,5376]{1,0:T(8,128)(2,1)} copy(bf16[96,5376]{1,0:T(8,128)(2,1)} %shard_map.109) | data formatting | bytes 2064384

commit v2 on v1

--- a/solution.py
+++ b/solution.py
@@ -19,6 +19,39 @@
 MESH = pl.DeviceIdType.MESH
 
 
+VIA_X = ()
+PLANS = {
+    (0, False): (
+        "SW", "Z1", "Z2", "R0", "R1", "R2", "Z3", "SO", "OWN", "W0", "W1", "A0",
+        "W2", "A1", "B0", "W3", "A2", "B1", "W4", "A3", "B2", "XZ", "W5", "A4",
+        "B3", "A5", "B4", "P1", "B5", "P2", "SC", "WC", "OB", "X1", "RN", "ON",
+        "KE", "X2", "Y1", "KV", "P3", "KX", "AT", "X3", "D1", "DZ", "Y2", "D2",
+        "Y3", "D3",
+    ),
+    (0, True): (
+        "SW", "R0", "R1", "R2", "Z1", "Z2", "Z3", "SO", "OWN", "W0", "W1", "A0",
+        "W2", "A1", "B0", "W3", "A2", "B1", "W4", "A3", "B2", "XZ", "W5", "A4",
+        "B3", "A5", "B4", "P1", "B5", "P2", "SC", "WC", "OB", "X1", "RN", "ON",
+        "KE", "X2", "Y1", "KV", "P3", "KX", "AT", "X3", "D1", "DZ", "Y2", "D2",
+        "Y3", "D3",
+    ),
+    (1, False): (
+        "R0", "SW", "Z1", "R1", "R2", "Z2", "Z3", "SO", "OWN", "W0", "W1", "A0",
+        "W2", "A1", "B0", "W3", "A2", "B1", "W4", "A3", "B2", "XZ", "W5", "A4",
+        "B3", "A5", "B4", "P1", "B5", "P2", "SC", "WC", "OB", "X1", "RN", "ON",
+        "KE", "X2", "Y1", "KV", "P3", "KX", "AT", "X3", "D1", "DZ", "Y2", "D2",
+        "Y3", "D3",
+    ),
+    (1, True): (
+        "SW", "SO", "OWN", "W0", "W1", "A0", "W2", "A1", "B0", "W3", "A2", "B1",
+        "W4", "A3", "B2", "XZ", "W5", "A4", "B3", "Z1", "R0", "R1", "R2", "Z2",
+        "Z3", "A5", "B4", "P1", "B5", "P2", "SC", "WC", "OB", "X1", "RN", "ON",
+        "KE", "X2", "Y1", "KV", "P3", "KX", "AT", "X3", "D1", "DZ", "Y2", "D2",
+        "Y3", "D3",
+    ),
+}
+
+
 def chunk_of(width, limit):
     best = 128
     for c in range(128, limit + 1, 128):
@@ -39,8 +72,8 @@
     lengths, tokens, wq_hbm, wkv_hbm, cache_hbm, oproj_hbm,
     ig_hbm, pg_hbm, qgain, kgain, freq,
     out_ref,
-    igs, pgs, igain, pgain, cos_t, sin_t, xbuf, nbuf, w, cbuf, og, q_all, kv_all, q_snd, kv_snd, hsnd, ho, proj,
-    lsem, s_w, s_x, s_c, s_o, s_oz, s_kvx, s_kv, s_q, s_h,
+    igs, pgs, igain, pgain, cos_t, sin_t, xbuf, nbuf, w, cbuf, og, q_all, kv_all, q_snd, kv_snd, hsnd, ho, proj, obuf,
+    lsem, osem, s_w, s_x, s_c, s_o, s_oz, s_kvx, s_kv, s_q, s_h,
     r_x, r_c, r_own, r_w, r_o, r_q, r_kv, r_kvx, r_h,
 ):
     t, s, z = lax.axis_index("tmpl"), lax.axis_index("seq"), lax.axis_index("tp")
@@ -114,35 +147,35 @@
     def piece(e_t, e_s, c):
         return pl.ds(pl.multiple_of((e_t * S2 + e_s) * DE + c * DN, DN), DN)
 
-    loc[1].wait()
-    loc[2].wait()
-
     def send_w():
         for c in range(NC):
             pc = piece(t, sb, c)
-            send(w.at[0, pc], w.at[1, pc], s_w, r_own.at[c], {"tp": zp})
+            for src, at in ((wq_hbm, pl.ds(0, HW)), (wkv_hbm, pl.ds(HW, 2 * HW))):
+                send(src.at[pc], w.at[1, pc, at], s_w, r_own.at[c], {"tp": zp})
 
     def send_rows(c):
         rows = pl.ds(c * RR, RR)
         for k in range(1, h):
             send(tokens.at[rows], xbuf.at[b, rows], s_x, r_x.at[b, c], {"tp": p * h + (b + k) % h})
 
-    @pl.when(par == 0)
-    def _():
-        send_w()
-        for c in range(RC):
-            send_rows(c)
-
-    @pl.when(par == 1)
-    def _():
-        send_rows(0)
-        send_w()
-        for c in range(1, RC):
-            send_rows(c)
-
-    for k in xs:
-        send(cache_hbm, cbuf.at[s], s_c, r_c.at[s], {"seq": k})
-
+    def o_copy(idx, dev):
+        send(og.at[idx], og.at[idx], s_o, r_o.at[idx], dev)
+
+    def z_out(n):
+        i = slab(s, t, z)
+        rows = pl.ds(pl.multiple_of(t * OR, OR), OR)
+        send(oproj_hbm.at[rows], og.at[i], s_oz, r_o.at[i], {"tp": n})
+
+    def z_to(d):
+        @pl.when(z + d < N)
+        def _():
+            z_out(jnp.minimum(z + d, N - 1))
+
+        @pl.when(z - d >= 0)
+        def _():
+            z_out(jnp.maximum(z - d, 0))
+
+    mid = (z == h - 1) | (z == h)
     lens = [lengths[k] for k in range(S)]
     offs = []
     total = jnp.int32(0)
@@ -198,62 +231,37 @@
         kv_all[s, n] = kv
         share(n)
 
-    def other_head(slot):
+    def other_head(slot, late=1):
         q, kv = project(slot, 1)
         n = p * h + slot
         q_snd[slot] = q
         kv_snd[slot] = kv
-        send(kv_snd.at[slot], kv_all.at[s, n], s_kv, r_kv, {"tp": zp})
+        send(kv_snd.at[slot], kv_all.at[s, n], s_kv, r_kv.at[late], {"tp": zp})
         send(q_snd.at[slot], q_all.at[n], s_q, r_q, {"tp": zp})
 
-    loc[3].wait()
-    loc[4].wait()
-    for k in range(D // 128):
-        igain[0:1, k * 128 : (k + 1) * 128] = igs[k : k + 1, :]
-        pgain[0:1, k * 128 : (k + 1) * 128] = pgs[k : k + 1, :]
-    lane = lax.broadcasted_iota(jnp.int32, (R, HW), 1)
-    for k in range(h):
-        row = lax.broadcasted_iota(jnp.int32, (R, HW), 0)
-        angle = (PREFIX + own_off + (p * h + k) * R + row).astype(F32) * freq[...]
-        cos_t[k] = jnp.cos(angle)
-        sine = jnp.sin(angle)
-        sin_t[k] = jnp.where(lane < HW // 2, -sine, sine)
-    loc[0].wait()
-    norm_rows(b, 0, R)
-    own_head(b)
-    for k in range(T):
-        loc[6 + k].wait()
-
-    def o_copy(idx, dev, ssem=None):
-        send(og.at[idx], og.at[idx], s_o if ssem is None else ssem, r_o.at[idx], dev)
-
-    def z_right(n):
-        @pl.when(z < N - 1)
-        def _():
-            o_copy(slab(s, t, n), {"tp": jnp.minimum(z + 1, N - 1)}, s_oz.at[n])
-
-    def z_left(n):
-        @pl.when(z > 0)
-        def _():
-            o_copy(slab(s, t, n), {"tp": jnp.maximum(z - 1, 0)}, s_oz.at[N + n])
-
-    def o_arrive(d):
-        @pl.when(z + d < N)
-        def _():
-            n = z + d
-            arrived(og.at[slab(s, t, n)], r_o.at[slab(s, t, n)])
-            z_left(n)
-            o_plane(n)
-
-        @pl.when(z - d >= 0)
-        def _():
-            n = z - d
-            arrived(og.at[slab(s, t, n)], r_o.at[slab(s, t, n)])
-            z_right(n)
-            o_plane(n)
-
-    def o_plane(n):
+    def tables():
+        loc[3].wait()
+        loc[4].wait()
+        for k in range(D // 128):
+            igain[0:1, k * 128 : (k + 1) * 128] = igs[k : k + 1, :]
+            pgain[0:1, k * 128 : (k + 1) * 128] = pgs[k : k + 1, :]
+        lane = lax.broadcasted_iota(jnp.int32, (R, HW), 1)
+        for k in range(h):
+            row = lax.broadcasted_iota(jnp.int32, (R, HW), 0)
+            angle = (PREFIX + own_off + (p * h + k) * R + row).astype(F32) * freq[...]
+            cos_t[k] = jnp.cos(angle)
+            sine = jnp.sin(angle)
+            sin_t[k] = jnp.where(lane < HW // 2, -sine, sine)
+        loc[0].wait()
+        norm_rows(b, 0, R)
+        loc[1].wait()
+        loc[2].wait()
+        own_head(b)
+        for k in range(T):
+            loc[6 + k].wait()
+    def plane(n):
         i = slab(s, t, n)
+        arrived(og.at[i], r_o.at[i])
         for k in xs:
             o_copy(i, {"seq": k})
         for k in ys:
@@ -269,122 +277,133 @@
         def _():
             fn(z - d)
 
-    def o_x(n):
+    def from_x(n, diag=True):
         for ks in xs:
             i = slab(ks, t, n)
             arrived(og.at[i], r_o.at[i])
-            for k in ys:
-                o_copy(i, {"tmpl": k})
+            if diag:
+                for k in ys:
+                    o_copy(i, {"tmpl": k})
             o_copy(i, {"tmpl": tc})
 
-    def o_y(n):
+    def from_y(n, diag=False):
         for kt in ys:
-            for ks in [s] + xs:
+            i = slab(s, kt, n)
+            arrived(og.at[i], r_o.at[i])
+            if diag:
+                for k in xs:
+                    o_copy(i, {"seq": k})
+            o_copy(i, {"tmpl": tc})
+
+    def from_diag(n):
+        for kt in ys:
+            for ks in xs:
                 i = slab(ks, kt, n)
                 arrived(og.at[i], r_o.at[i])
                 o_copy(i, {"tmpl": tc})
 
-    def o_last(n):
+    def from_c(n, own=False):
         for kt in cross:
-            for ks in [s] + xs:
+            for ks in xs if own else [s] + xs:
                 i = slab(ks, kt, n)
                 arrived(og.at[i], r_o.at[i])
 
-    def own_x():
-        for kt in same:
-            for k in xs:
-                o_copy(slab(s, kt, z), {"seq": k})
-
-    def own_c():
-        for ks in xs:
-            for kt in same:
-                i = slab(ks, kt, z)
-                arrived(og.at[i], r_o.at[i])
-                o_copy(i, {"tmpl": tc})
-
-    def own_last():
-        for ks in xs:
-            for kt in cross:
-                i = slab(ks, kt, z)
-                arrived(og.at[i], r_o.at[i])
-
-    z_right(z)
-    z_left(z)
+    def w_send(e_t, e_s, c, dev):
+        pc = piece(e_t, e_s, c)
+        send(w.at[1, pc], w.at[1, pc], s_w, r_w.at[e_t, e_s, c], dev)
 
     def w_own(c):
-        pc = piece(t, sb, c)
-        arrived(w.at[1, pc], r_own.at[c])
+        arrived(w.at[1, piece(t, sb, c)], r_own.at[c])
         for k in x2:
-            send(w.at[1, pc], w.at[1, pc], s_w, r_w.at[t, sb, c], {"seq": sg + k})
+            w_send(t, sb, c, {"seq": sg + k})
         for k in ys:
-            send(w.at[1, pc], w.at[1, pc], s_w, r_w.at[t, sb, c], {"tmpl": k})
-        send(w.at[1, pc], w.at[1, pc], s_w, r_w.at[t, sb, c], {"tmpl": tc})
-
-    def w_x(c):
+            w_send(t, sb, c, {"tmpl": k})
+        w_send(t, sb, c, {"tmpl": tc})
+
+    def w_got(e_t, e_s, c):
+        arrived(w.at[1, piece(e_t, e_s, c)], r_w.at[e_t, e_s, c])
+
+    def w_one(c):
         for k2 in x2:
-            pc = piece(t, k2, c)
-            arrived(w.at[1, pc], r_w.at[t, k2, c])
-            for k in ys:
-                send(w.at[1, pc], w.at[1, pc], s_w, r_w.at[t, k2, c], {"tmpl": k})
-            send(w.at[1, pc], w.at[1, pc], s_w, r_w.at[t, k2, c], {"tmpl": tc})
-
-    def w_y(c):
-        for k in ys:
-            for ks in range(S2):
-                pc = piece(k, ks, c)
-                arrived(w.at[1, pc], r_w.at[k, ks, c])
-                send(w.at[1, pc], w.at[1, pc], s_w, r_w.at[k, ks, c], {"tmpl": tc})
-
-    for i in range(NC + 1):
-        if i < NC:
-            w_own(i)
-        if i > 0:
-            w_x(i - 1)
-    own_x()
-    for c in range(NC):
-        w_y(c)
-    for c in range(NC):
-        for kt in cross:
-            for ks in range(S2):
-                arrived(w.at[1, piece(kt, ks, c)], r_w.at[kt, ks, c])
-    other_head(b)
-    for k in range(1, h):
-        slot = (b + k) % h
+            w_got(t, k2, c)
+            if c % 2 == 0:
+                for k in ys:
+                    w_send(t, k2, c, {"tmpl": k})
+            w_send(t, k2, c, {"tmpl": tc})
+        for kt in ys:
+            w_got(kt, sb, c)
+            if c % 2 == 1:
+                for k in x2:
+                    w_send(kt, sb, c, {"seq": sg + k})
+            w_send(kt, sb, c, {"tmpl": tc})
+
+    def w_two(c):
+        for kt in ys:
+            for k2 in x2:
+                w_got(kt, k2, c)
+                w_send(kt, k2, c, {"tmpl": tc})
+
+    def take_rows(slot):
         for c in range(RC):
             rows = pl.ds(c * RR, RR)
             arrived(xbuf.at[slot, rows], r_x.at[slot, c])
             norm_rows(slot, c * RR, RR)
-        other_head(slot)
-    for k in range(1, h):
-        own_head((b + k) % h)
-
-    own_c()
-    o_arrive(1)
-    arrived(kv_all.at[s, pl.ds(op * h, h)], r_kv)
-    for i in range(h):
-        share(op * h + i)
-    arrived(q_all.at[pl.ds(op * h, h)], r_q)
-    each(1, o_x)
-    loc[5].wait()
-    for k in xs:
-        arrived(cbuf.at[k], r_c.at[k])
-        arrived(kv_all.at[k], r_kvx.at[k])
+
+    def w_cross():
+        for c in range(NC):
+            for kt in cross:
+                for ks in range(S2):
+                    w_got(kt, ks, c)
+
+    def send_cache():
+        for k in xs:
+            send(cache_hbm, cbuf.at[s], s_c, r_c.at[s], {"seq": k})
+
+    def send_own():
+        rows = pl.ds(pl.multiple_of(t * OR, OR), OR)
+        i = slab(s, t, z)
+        for k in xs:
+            send(oproj_hbm.at[rows], og.at[i], s_o, r_o.at[i], {"seq": k})
+
+    def other_rows():
+        for k in range(1, h):
+            take_rows((b + k) % h)
+            other_head((b + k) % h)
+
+    def own_rows():
+        for k in range(1, h):
+            own_head((b + k) % h)
+
+    def wait_early():
+        n = op * h + b
+        arrived(kv_all.at[s, n], r_kv.at[0])
+        share(n)
+
+    def wait_kv():
+        arrived(kv_all.at[s, pl.ds(op * h, h - 1)], r_kv.at[1])
+        for k in range(1, h):
+            share(op * h + (b + k) % h)
+        arrived(q_all.at[pl.ds(op * h, h)], r_q)
+
+    def wait_kvx():
+        loc[5].wait()
+        for k in xs:
+            arrived(cbuf.at[k], r_c.at[k])
+            arrived(kv_all.at[k], r_kvx.at[k])
 
     def attend(d, carry):
         n = lax.rem(z + d, N)
         q = q_all[n]
         slot_c = n * R + lax.broadcasted_iota(jnp.int32, (R, 1), 0)
         pos = PREFIX + own_off + slot_c
-        scores, allow, values = [], [], []
+        scores, values = [], []
         for k in range(S):
             cb = cbuf[k]
             sc = lax.dot_general(
                 q, cb[:, :HW], (((1,), (1,)), ((), ())), preferred_element_type=F32
             )
             kp = PREFIX - WIN + k * C + lax.broadcasted_iota(jnp.int32, (1, C), 1)
-            ok = (kp <= pos) & (kp > pos - WIN)
-            scores.append(jnp.where(ok, sc, MASKED))
-            allow.append(ok)
+            scores.append(jnp.where(kp > pos - WIN, sc, MASKED))
             values.append(cb[:, HW:])
             kv = flat(kv_all[k])
             sc = lax.dot_general(
@@ -392,17 +411,19 @@
             )
             j = lax.broadcasted_iota(jnp.int32, (1, N * R), 1)
             kp = PREFIX + offs[k] + j
-            ok = (kp <= pos) & (kp > pos - WIN) & (j < lens[k])
+            kp = jnp.where(j < lens[k], kp, PREFIX + WIN + S * N * R)
+            ok = kp <= pos
+            if S * N * R > WIN:
+                ok = ok & (kp > pos - WIN)
             scores.append(jnp.where(ok, sc, MASKED))
-            allow.append(ok)
             values.append(kv[:, HW:])
         top = functools.reduce(
             jnp.maximum, [jnp.max(v, axis=1, keepdims=True) for v in scores]
         )
         row_sum = jnp.zeros((R, 1), F32)
         acc = jnp.zeros((R, HW), F32)
-        for sc, ok, vv in zip(scores, allow, values):
-            wt = jnp.where(ok, jnp.exp(sc - top), 0.0)
+        for sc, vv in zip(scores, values):
+            wt = jnp.exp(sc - top)
             row_sum = row_sum + jnp.sum(wt, axis=1, keepdims=True)
             acc = acc + jnp.dot(wt.astype(BF16), vv, preferred_element_type=F32)
         live = slot_c < own_len
@@ -415,29 +436,85 @@
 
         return carry
 
-    lax.fori_loop(1, N + 1, attend, 0)
-    ho[z] = hsnd[z]
-
-    for d in range(2, N):
-        o_arrive(d)
-        each(d - 1, o_y)
-        each(d, o_x)
-    each(N - 1, o_y)
-    own_last()
+    def attention():
+        lax.fori_loop(1, N + 1, attend, 0)
+        ho[z] = hsnd[z]
+
+    def dist(k):
+        return [d for d in range(1, N) if d == k or (k == 3 and d > 3)]
+
+    ops = {
+        "SW": send_w, "OWN": tables, "SC": send_cache, "SO": send_own, "WC": w_cross,
+        "OB": lambda: other_head(b, 0), "KE": wait_early, "RN": other_rows, "ON": own_rows, "KV": wait_kv,
+        "KX": wait_kvx, "AT": attention, "XZ": lambda: from_x(z), "DZ": lambda: from_diag(z),
+    }
+
+    def step(tok):
+        if tok in ops:
+            return ops[tok]()
+        kind, k = tok[0], int(tok[1])
+        if kind in "WAB":
+            if k < NC:
+                (w_own if kind == "W" else w_one if kind == "A" else w_two)(k)
+        elif kind == "R":
+            if k < RC:
+                send_rows(k)
+        else:
+            via_x = k in VIA_X
+            for d in dist(k):
+                if kind == "Z":
+                    z_to(d)
+                elif kind == "P":
+                    each(d, plane)
+                elif kind == "X":
+                    each(d, lambda n: from_x(n, not via_x))
+                elif kind == "Y":
+                    each(d, lambda n: from_y(n, via_x))
+                elif kind == "D":
+                    each(d, from_diag)
+
+    kinds = [(0, False), (0, True), (1, False), (1, True)]
+    plans = [PLANS[k] for k in kinds]
+    first = 0
+    while all(len(q) > first and q[first] == plans[0][first] for q in plans):
+        step(plans[0][first])
+        first += 1
+    last = 0
+    while all(len(q) > first + last and q[-1 - last] == plans[0][-1 - last] for q in plans):
+        last += 1
+    for (kp, km), q in zip(kinds, plans):
+        if len(q) > first + last:
+            @pl.when((par == kp) & (mid == km))
+            def _():
+                for tok in q[first : len(q) - last]:
+                    step(tok)
+    for tok in plans[0][len(plans[0]) - last :]:
+        step(tok)
+    from_c(z, True)
     for d in range(1, N):
-        each(d, o_last)
+        each(d, from_c)
     arrived(ho.at[pl.ds(0, N - 1)], r_h)
 
     CC = chunk_of(DC, 1024)
+
+    def partial(first, k, cs):
+        acc = None
+        for g in range(0, h, 2):
+            n = first + g
+            wt = jnp.concatenate(
+                [og[slab(k, kt, n + j), :, cs] for j in range(2) for kt in range(T)], axis=0
+            )
+            hv = jnp.concatenate([ho[n + j] for j in range(2)], axis=1)
+            v = jnp.dot(hv, wt, preferred_element_type=F32)
+            acc = v if acc is None else acc + v
+        return acc
 
     for k in range(S):
         def cols(i, carry):
             cs = pl.ds(pl.multiple_of(i * CC, CC), CC)
-            acc = jnp.zeros((R, CC), F32)
-            for g in range(N):
-                wt = jnp.concatenate([og[slab(k, kt, g), :, cs] for kt in range(T)], axis=0)
-                acc = acc + jnp.dot(ho[g], wt, preferred_element_type=F32).astype(BF16).astype(F32)
-            proj[:, pl.ds(pl.multiple_of(k * DC + i * CC, 128), CC)] = acc
+            proj[:, pl.ds(pl.multiple_of(k * DC + i * CC, 128), CC)] = (
+                partial(p * h, k, cs) + partial(op * h, k, cs)
+            )
             return carry
 
         lax.fori_loop(0, DC // CC, cols, 0)
@@ -448,11 +525,13 @@
         rows = pl.ds(pl.multiple_of(i * RF, RF), RF)
         v = proj[rows, :]
         inv = lax.rsqrt(jnp.sum(v * v, axis=1, keepdims=True) * (1.0 / D) + EPSILON)
-        out_ref[rows, :] = (xbuf[b, rows, :].astype(F32) + v * inv * pgain[...]).astype(BF16)
+        obuf[rows, :] = (xbuf[b, rows, :].astype(F32) + v * inv * pgain[...]).astype(BF16)
+        pltpu.make_async_copy(obuf.at[rows], out_ref.at[rows], osem).start()
         return carry
 
     lax.fori_loop(0, R // RF, finish, 0)
 
+    pltpu.make_async_copy(obuf, out_ref, osem).wait()
     left(w.at[1], s_w)
     left(xbuf.at[pl.ds(0, h - 1)], s_x)
     left(cbuf.at[pl.ds(0, S - 1)], s_c)
@@ -466,14 +545,7 @@
         part = min(count, S * T * N)
         left(og.at[pl.ds(0, part)], s_o)
         count -= part
-    for n in range(N):
-        @pl.when((n <= z) & (z < N - 1))
-        def _():
-            left(og.at[0], s_oz.at[n])
-
-        @pl.when((n >= z) & (z > 0))
-        def _():
-            left(og.at[0], s_oz.at[N + n])
+    left(og.at[pl.ds(0, N - 1)], s_oz)
 
 
 def shards(
@@ -486,7 +558,7 @@
     C = window_cache.shape[0]
     h = N // 2
     S2 = max(d for d in range(1, S + 1) if S % d == 0 and D % (16 * T * d) == 0)
-    NC = max(d for d in (1, 2, 3) if D // (T * S2) % (16 * d) == 0)
+    NC = max(d for d in (1, 2, 3, 6) if D // (T * S2) % (16 * d) == 0)
     RC = 3 if R % 48 == 0 else 1
     inv = np.power(ROPE_BASE, -2.0 * np.arange(HW // 2) / HW)
     freq = np.concatenate([inv, inv])[None, :].astype(np.float32)
@@ -499,7 +571,7 @@
         out_shape=jax.ShapeDtypeStruct((R, D), BF16),
         in_specs=[pl.BlockSpec(memory_space=pltpu.SMEM), hb, hb, hb, hb, hb]
         + [hb, hb, vm, vm, vm],
-        out_specs=vm,
+        out_specs=hb,
         scratch_shapes=[
             pltpu.VMEM((D // 128, 128), F32),
             pltpu.VMEM((D // 128, 128), F32),
@@ -519,12 +591,13 @@
             pltpu.VMEM((N, R, HW), BF16),
             pltpu.VMEM((N, R, HW), BF16),
             pltpu.VMEM((R, D), F32),
-            dma((6 + T,)), dma, dma, dma, dma, dma((2 * N,)), dma, dma, dma, dma,
+            pltpu.VMEM((R, D), BF16),
+            dma((6 + T,)), dma, dma, dma, dma, dma, dma, dma, dma, dma, dma,
             dma((h, RC)), dma((S,)), dma((NC,)), dma((T, S2, NC)), dma((S * T * N,)),
-            dma, dma, dma((S,)), dma,
+            dma, dma((2,)), dma((S,)), dma,
         ],
         compiler_params=pltpu.CompilerParams(
-            collective_id=0, has_side_effects=True, vmem_limit_bytes=67043328 - 2 * R * D * 2
+            collective_id=0, has_side_effects=True, vmem_limit_bytes=67043328 - R * D * 2
         ),
     )(
         lengths, tokens, query_proj, key_value, window_cache, output_proj,

time: 90.3 us -> 77.8 us (0.86)
  Pallas kernels: 87.3 us -> 75.4 us
    pallas_call x1, Pallas kernels: 87.3 us -> 75.4 us  [shards(): pl.pallas_call(functools.partial(kernel, T, S, N, S2, NC, RC), out_shape=...]
where the time goes in v2:
time: 77.8 us; the launch traced here: 77.6 us
  Pallas kernels  75.4 us (97%)
  local copies, waits for them, and re-layouts  2.25 us (3%)
    pallas_call x1, Pallas kernels, shards(): pl.pallas_call(functools.partial(kernel, T, S, N, S2, NC, RC), out_shape=...  75.4 us
    unnamed x1, local copies, waits for them, and re-layouts  2.25 us

profile of v2, /device:TPU:0, one launch (start us, length us, event | category | flops | bytes accessed | tf_op | source)
XLA Modules:
  0.0 77.6 jit_solution(11020766785763346558)
XLA Ops:
  0.0 75.4 %shard_map.109 = bf16[96,5376]{1,0:T(8,128)(2,1)} custom-call(s32[2]{0:T(128)} %lengths.1, bf16[96,5376]{1,0:T(8,128)(2,1)} %tokens.1, bf16[5376,128]{1,0:T(8,128)(2,1)} %wq_hbm.1, bf16[5376,256]{1,0:T(8,128)(2,1)} %wkv_hbm.1, bf16[512,256]{1,0:T(8,128)(2,1)} %cache_hbm.1, bf16[128,2688]{1,0:T(8,128)(2,1)} %oproj_hbm.1, f32[42,128]{1,0:T(8,128)} %bitcast.4, ...), custom_call_target="tpu_custom_call" | custom-call | tf_op jit(solution)/shard_map/pallas_call | solution.py:569
  75.4 2.2 %copy.13 = bf16[96,5376]{1,0:T(8,128)(2,1)} copy(bf16[96,5376]{1,0:T(8,128)(2,1)} %shard_map.109) | data formatting | bytes 2064384

commit v3 on v2

--- a/solution.py
+++ b/solution.py
@@ -22,31 +22,31 @@
 VIA_X = ()
 PLANS = {
     (0, False): (
-        "SW", "Z1", "Z2", "R0", "R1", "R2", "Z3", "SO", "OWN", "W0", "W1", "A0",
-        "W2", "A1", "B0", "W3", "A2", "B1", "W4", "A3", "B2", "XZ", "W5", "A4",
-        "B3", "A5", "B4", "P1", "B5", "P2", "SC", "WC", "OB", "X1", "RN", "ON",
-        "KE", "X2", "Y1", "KV", "P3", "KX", "AT", "X3", "D1", "DZ", "Y2", "D2",
+        "SW", "Z1", "R0", "R1", "Z2", "R2", "Z3", "SO", "SC", "W0", "OWN", "W1",
+        "A0", "W2", "A1", "B0", "W3", "A2", "B1", "W4", "A3", "B2", "XZ", "W5",
+        "A4", "B3", "A5", "B4", "P1", "B5", "P2", "WC", "OB", "RN", "X1", "ON",
+        "KE", "X2", "P3", "Y1", "KV", "X3", "KX", "AT", "D1", "DZ", "Y2", "D2",
         "Y3", "D3",
     ),
     (0, True): (
         "SW", "R0", "R1", "R2", "Z1", "Z2", "Z3", "SO", "OWN", "W0", "W1", "A0",
         "W2", "A1", "B0", "W3", "A2", "B1", "W4", "A3", "B2", "XZ", "W5", "A4",
-        "B3", "A5", "B4", "P1", "B5", "P2", "SC", "WC", "OB", "X1", "RN", "ON",
-        "KE", "X2", "Y1", "KV", "P3", "KX", "AT", "X3", "D1", "DZ", "Y2", "D2",
+        "B3", "A5", "B4", "P1", "B5", "SC", "WC", "OB", "X1", "RN", "P2", "P3",
+        "ON", "KE", "Y1", "KV", "X2", "X3", "KX", "AT", "D1", "DZ", "Y2", "D2",
         "Y3", "D3",
     ),
     (1, False): (
-        "R0", "SW", "Z1", "R1", "R2", "Z2", "Z3", "SO", "OWN", "W0", "W1", "A0",
-        "W2", "A1", "B0", "W3", "A2", "B1", "W4", "A3", "B2", "XZ", "W5", "A4",
-        "B3", "A5", "B4", "P1", "B5", "P2", "SC", "WC", "OB", "X1", "RN", "ON",
-        "KE", "X2", "Y1", "KV", "P3", "KX", "AT", "X3", "D1", "DZ", "Y2", "D2",
+        "R0", "SW", "Z1", "R1", "R2", "Z2", "SO", "SC", "W0", "W1", "A0", "W2",
+        "A1", "B0", "OWN", "W3", "A2", "B1", "W4", "A3", "B2", "XZ", "W5", "A4",
+        "B3", "A5", "B4", "P1", "B5", "P2", "WC", "OB", "Z3", "KE", "X1", "X2",
+        "RN", "ON", "Y1", "KV", "P3", "KX", "X3", "AT", "D1", "DZ", "Y2", "D2",
         "Y3", "D3",
     ),
     (1, True): (
         "SW", "SO", "OWN", "W0", "W1", "A0", "W2", "A1", "B0", "W3", "A2", "B1",
         "W4", "A3", "B2", "XZ", "W5", "A4", "B3", "Z1", "R0", "R1", "R2", "Z2",
-        "Z3", "A5", "B4", "P1", "B5", "P2", "SC", "WC", "OB", "X1", "RN", "ON",
-        "KE", "X2", "Y1", "KV", "P3", "KX", "AT", "X3", "D1", "DZ", "Y2", "D2",
+        "Z3", "A5", "B4", "P1", "B5", "SC", "WC", "OB", "X1", "RN", "P2", "P3",
+        "ON", "KE", "Y1", "KV", "X2", "X3", "KX", "AT", "D1", "DZ", "Y2", "D2",
         "Y3", "D3",
     ),
 }
@@ -74,7 +74,7 @@
     out_ref,
     igs, pgs, igain, pgain, cos_t, sin_t, xbuf, nbuf, w, cbuf, og, q_all, kv_all, q_snd, kv_snd, hsnd, ho, proj, obuf,
     lsem, osem, s_w, s_x, s_c, s_o, s_oz, s_kvx, s_kv, s_q, s_h,
-    r_x, r_c, r_own, r_w, r_o, r_q, r_kv, r_kvx, r_h,
+    r_x, r_c, r_own, r_w, r_wc, r_o, r_oc, r_q, r_kv, r_kvx, r_h,
 ):
     t, s, z = lax.axis_index("tmpl"), lax.axis_index("seq"), lax.axis_index("tp")
     h = N // 2
@@ -92,8 +92,6 @@
     tc = t + 1 - 2 * (t % 2)
     par = t % 2
     ys = [(t + 2 * k) % T for k in range(1, T // 2)]
-    same = [t] + ys
-    cross = [(tc + 2 * k) % T for k in range(T // 2)]
     xs = [(s + k) % S for k in range(1, S)]
     sg, sb = (s // S2) * S2, s % S2
     x2 = [(sb + k) % S2 for k in range(1, S2)]
@@ -126,10 +124,13 @@
     def slab(ks, kt, n):
         return (ks * T + kt) * N + n
 
+    def slot_of(ks, kt, n):
+        return (ks * (T // 2) + kt // 2) * N + n
+
     for k in range(T):
         loc.append(
             pltpu.make_async_copy(
-                oproj_hbm.at[pl.ds(k * OR, OR)], og.at[slab(s, k, z)], lsem.at[6 + k]
+                oproj_hbm.at[pl.ds(k * OR, OR)], og.at[slab(s, k, z)], lsem.at[6]
             )
         )
     for c in loc:
@@ -158,13 +159,22 @@
         for k in range(1, h):
             send(tokens.at[rows], xbuf.at[b, rows], s_x, r_x.at[b, c], {"tp": p * h + (b + k) % h})
 
-    def o_copy(idx, dev):
-        send(og.at[idx], og.at[idx], s_o, r_o.at[idx], dev)
+    pt = jnp.where(z < h, jnp.where(z == h - 1, h, h - 1), jnp.where(z == h, h - 1, h))
+
+    def o_copy(ks, kt, n, dev):
+        i = slab(ks, kt, n)
+        if "tmpl" in dev and dev["tmpl"] is tc:
+            sem = r_oc.at[jnp.where((n == z) | (n == pt), 0, 1)]
+        else:
+            sem = r_o.at[slot_of(ks, kt, n)]
+        send(og.at[i], og.at[i], s_o, sem, dev)
+
+    def o_got(ks, kt, n):
+        arrived(og.at[slab(ks, kt, n)], r_o.at[slot_of(ks, kt, n)])
 
     def z_out(n):
-        i = slab(s, t, z)
         rows = pl.ds(pl.multiple_of(t * OR, OR), OR)
-        send(oproj_hbm.at[rows], og.at[i], s_oz, r_o.at[i], {"tp": n})
+        send(oproj_hbm.at[rows], og.at[slab(s, t, z)], s_oz, r_o.at[slot_of(s, t, z)], {"tp": n})
 
     def z_to(d):
         @pl.when(z + d < N)
@@ -257,16 +267,14 @@
         loc[1].wait()
         loc[2].wait()
         own_head(b)
-        for k in range(T):
-            loc[6 + k].wait()
+        pltpu.make_async_copy(og.at[pl.ds(0, T)], og.at[pl.ds(0, T)], lsem.at[6]).wait()
     def plane(n):
-        i = slab(s, t, n)
-        arrived(og.at[i], r_o.at[i])
+        o_got(s, t, n)
         for k in xs:
-            o_copy(i, {"seq": k})
+            o_copy(s, t, n, {"seq": k})
         for k in ys:
-            o_copy(i, {"tmpl": k})
-        o_copy(i, {"tmpl": tc})
+            o_copy(s, t, n, {"tmpl": k})
+        o_copy(s, t, n, {"tmpl": tc})
 
     def each(d, fn):
         @pl.when(z + d < N)
@@ -279,38 +287,30 @@
 
     def from_x(n, diag=True):
         for ks in xs:
-            i = slab(ks, t, n)
-            arrived(og.at[i], r_o.at[i])
+            o_got(ks, t, n)
             if diag:
                 for k in ys:
-                    o_copy(i, {"tmpl": k})
-            o_copy(i, {"tmpl": tc})
+                    o_copy(ks, t, n, {"tmpl": k})
+            o_copy(ks, t, n, {"tmpl": tc})
 
     def from_y(n, diag=False):
         for kt in ys:
-            i = slab(s, kt, n)
-            arrived(og.at[i], r_o.at[i])
+            o_got(s, kt, n)
             if diag:
                 for k in xs:
-                    o_copy(i, {"seq": k})
-            o_copy(i, {"tmpl": tc})
+                    o_copy(s, kt, n, {"seq": k})
+            o_copy(s, kt, n, {"tmpl": tc})
 
     def from_diag(n):
         for kt in ys:
             for ks in xs:
-                i = slab(ks, kt, n)
-                arrived(og.at[i], r_o.at[i])
-                o_copy(i, {"tmpl": tc})
-
-    def from_c(n, own=False):
-        for kt in cross:
-            for ks in xs if own else [s] + xs:
-                i = slab(ks, kt, n)
-                arrived(og.at[i], r_o.at[i])
+                o_got(ks, kt, n)
+                o_copy(ks, kt, n, {"tmpl": tc})
 
     def w_send(e_t, e_s, c, dev):
         pc = piece(e_t, e_s, c)
-        send(w.at[1, pc], w.at[1, pc], s_w, r_w.at[e_t, e_s, c], dev)
+        sem = r_wc if "tmpl" in dev and dev["tmpl"] is tc else r_w.at[e_t // 2, e_s, c]
+        send(w.at[1, pc], w.at[1, pc], s_w, sem, dev)
 
     def w_own(c):
         arrived(w.at[1, piece(t, sb, c)], r_own.at[c])
@@ -321,7 +321,7 @@
         w_send(t, sb, c, {"tmpl": tc})
 
     def w_got(e_t, e_s, c):
-        arrived(w.at[1, piece(e_t, e_s, c)], r_w.at[e_t, e_s, c])
+        arrived(w.at[1, piece(e_t, e_s, c)], r_w.at[e_t // 2, e_s, c])
 
     def w_one(c):
         for k2 in x2:
@@ -350,10 +350,7 @@
             norm_rows(slot, c * RR, RR)
 
     def w_cross():
-        for c in range(NC):
-            for kt in cross:
-                for ks in range(S2):
-                    w_got(kt, ks, c)
+        arrived(w.at[1, pl.ds(0, D // 2)], r_wc)
 
     def send_cache():
         for k in xs:
@@ -363,7 +360,7 @@
         rows = pl.ds(pl.multiple_of(t * OR, OR), OR)
         i = slab(s, t, z)
         for k in xs:
-            send(oproj_hbm.at[rows], og.at[i], s_o, r_o.at[i], {"seq": k})
+            send(oproj_hbm.at[rows], og.at[i], s_o, r_o.at[slot_of(s, t, z)], {"seq": k})
 
     def other_rows():
         for k in range(1, h):
@@ -392,9 +389,9 @@
             arrived(kv_all.at[k], r_kvx.at[k])
 
     def attend(d, carry):
-        n = lax.rem(z + d, N)
-        q = q_all[n]
-        slot_c = n * R + lax.broadcasted_iota(jnp.int32, (R, 1), 0)
+        m = lax.rem(z // 2 + d, h)
+        q = flat(q_all[pl.ds(2 * m, 2)])
+        slot_c = 2 * m * R + lax.broadcasted_iota(jnp.int32, (2 * R, 1), 0)
         pos = PREFIX + own_off + slot_c
         scores, values = [], []
         for k in range(S):
@@ -420,24 +417,28 @@
         top = functools.reduce(
             jnp.maximum, [jnp.max(v, axis=1, keepdims=True) for v in scores]
         )
-        row_sum = jnp.zeros((R, 1), F32)
-        acc = jnp.zeros((R, HW), F32)
+        row_sum = jnp.zeros((2 * R, 1), F32)
+        acc = jnp.zeros((2 * R, HW), F32)
         for sc, vv in zip(scores, values):
             wt = jnp.exp(sc - top)
             row_sum = row_sum + jnp.sum(wt, axis=1, keepdims=True)
             acc = acc + jnp.dot(wt.astype(BF16), vv, preferred_element_type=F32)
         live = slot_c < own_len
         res = acc / jnp.where(live, row_sum, 1.0)
-        hsnd[n] = jnp.where(live, res, 0.0).astype(BF16)
-
-        @pl.when(d < N)
-        def _():
-            send(hsnd.at[n], ho.at[z], s_h, r_h, {"tp": n})
+        res = jnp.where(live, res, 0.0).astype(BF16)
+        for j in range(2):
+            hsnd[2 * m + j] = res[j * R : (j + 1) * R]
+        for j in range(2):
+            n = 2 * m + j
+
+            @pl.when(n != z)
+            def _():
+                send(hsnd.at[n], ho.at[z], s_h, r_h.at[z], {"tp": n})
 
         return carry
 
     def attention():
-        lax.fori_loop(1, N + 1, attend, 0)
+        lax.fori_loop(1, h + 1, attend, 0)
         ho[z] = hsnd[z]
 
     def dist(k):
@@ -490,34 +491,38 @@
                     step(tok)
     for tok in plans[0][len(plans[0]) - last :]:
         step(tok)
-    from_c(z, True)
-    for d in range(1, N):
-        each(d, from_c)
-    arrived(ho.at[pl.ds(0, N - 1)], r_h)
-
     CC = chunk_of(DC, 1024)
-
-    def partial(first, k, cs):
-        acc = None
-        for g in range(0, h, 2):
-            n = first + g
-            wt = jnp.concatenate(
-                [og[slab(k, kt, n + j), :, cs] for j in range(2) for kt in range(T)], axis=0
-            )
-            hv = jnp.concatenate([ho[n + j] for j in range(2)], axis=1)
-            v = jnp.dot(hv, wt, preferred_element_type=F32)
-            acc = v if acc is None else acc + v
-        return acc
-
-    for k in range(S):
-        def cols(i, carry):
-            cs = pl.ds(pl.multiple_of(i * CC, CC), CC)
-            proj[:, pl.ds(pl.multiple_of(k * DC + i * CC, 128), CC)] = (
-                partial(p * h, k, cs) + partial(op * h, k, cs)
-            )
-            return carry
-
-        lax.fori_loop(0, DC // CC, cols, 0)
+    lo, hi = jnp.minimum(z, pt), jnp.maximum(z, pt)
+    rest = []
+    for j in range(N - 2):
+        n = j + jnp.where(j >= lo, 1, 0)
+        rest.append(n + jnp.where(n >= hi, 1, 0))
+
+    def project_out(pair, more):
+        hv = jnp.concatenate([ho[n] for n in pair], axis=1)
+        for k in range(S):
+            def cols(i, carry):
+                cs = pl.ds(pl.multiple_of(i * CC, CC), CC)
+                at = pl.ds(pl.multiple_of(k * DC + i * CC, 128), CC)
+                wt = jnp.concatenate(
+                    [og[slab(k, kt, n), :, cs] for n in pair for kt in range(T)], axis=0
+                )
+                v = jnp.dot(hv, wt, preferred_element_type=F32)
+                proj[:, at] = proj[:, at] + v if more else v
+                return carry
+
+            lax.fori_loop(0, DC // CC, cols, 0)
+
+    X, Y = S - 1, T // 2 - 1
+    near = (X + S) * (T // 2)
+    arrived(og.at[pl.ds(0, near)], r_oc.at[0])
+    arrived(ho.at[pt], r_h.at[pt])
+    project_out([z, pt], False)
+    arrived(og.at[pl.ds(0, (N - 2) * S * (T // 2))], r_oc.at[1])
+    for n in rest:
+        arrived(ho.at[n], r_h.at[n])
+    for j in range(0, N - 2, 2):
+        project_out(rest[j : j + 2], True)
 
     RF = 16 if R % 16 == 0 else 8
 
@@ -539,7 +544,6 @@
     left(kv_snd, s_kv)
     left(q_snd, s_q)
     left(hsnd.at[pl.ds(0, N - 1)], s_h)
-    X, Y = S - 1, T // 2 - 1
     count = (N - 1) * (X + Y + 1 + X * (Y + 1) + Y * S) + (Y + 1) * X * 2
     while count > 0:
         part = min(count, S * T * N)
@@ -592,9 +596,9 @@
             pltpu.VMEM((N, R, HW), BF16),
             pltpu.VMEM((R, D), F32),
             pltpu.VMEM((R, D), BF16),
-            dma((6 + T,)), dma, dma, dma, dma, dma, dma, dma, dma, dma, dma,
-            dma((h, RC)), dma((S,)), dma((NC,)), dma((T, S2, NC)), dma((S * T * N,)),
-            dma, dma((2,)), dma((S,)), dma,
+            dma((7,)), dma, dma, dma, dma, dma, dma, dma, dma, dma, dma,
+            dma((h, RC)), dma((S,)), dma((NC,)), dma((T // 2, S2, NC)), dma, dma((S * T // 2 * N,)), dma((2,)),
+            dma, dma((2,)), dma((S,)), dma((N,)),
         ],
         compiler_params=pltpu.CompilerParams(
             collective_id=0, has_side_effects=True, vmem_limit_bytes=67043328 - R * D * 2

time: 77.8 us -> 73.2 us (0.941)
  Pallas kernels: 75.4 us -> 70.8 us
    pallas_call x1, Pallas kernels: 75.4 us -> 70.8 us  [shards(): pl.pallas_call(functools.partial(kernel, T, S, N, S2, NC, RC), out_shape=...]
where the time goes in v3:
time: 73.2 us; the launch traced here: 73 us
  Pallas kernels  70.8 us (97%)
  local copies, waits for them, and re-layouts  2.25 us (3%)
    pallas_call x1, Pallas kernels, shards(): pl.pallas_call(functools.partial(kernel, T, S, N, S2, NC, RC), out_shape=...  70.8 us
    unnamed x1, local copies, waits for them, and re-layouts  2.25 us

profile of v3, /device:TPU:0, one launch (start us, length us, event | category | flops | bytes accessed | tf_op | source)
XLA Modules:
  0.0 73.0 jit_solution(12888883622341564176)
XLA Ops:
  0.0 70.8 %shard_map.109 = bf16[96,5376]{1,0:T(8,128)(2,1)} custom-call(s32[2]{0:T(128)} %lengths.1, bf16[96,5376]{1,0:T(8,128)(2,1)} %tokens.1, bf16[5376,128]{1,0:T(8,128)(2,1)} %wq_hbm.1, bf16[5376,256]{1,0:T(8,128)(2,1)} %wkv_hbm.1, bf16[512,256]{1,0:T(8,128)(2,1)} %cache_hbm.1, bf16[128,2688]{1,0:T(8,128)(2,1)} %oproj_hbm.1, f32[42,128]{1,0:T(8,128)} %bitcast.4, ...), custom_call_target="tpu_custom_call" | custom-call | tf_op jit(solution)/shard_map/pallas_call | solution.py:573
  70.8 2.2 %copy.13 = bf16[96,5376]{1,0:T(8,128)(2,1)} copy(bf16[96,5376]{1,0:T(8,128)(2,1)} %shard_map.109) | data formatting | bytes 2064384

commit v4 on v3

--- a/solution.py
+++ b/solution.py
@@ -19,7 +19,7 @@
 MESH = pl.DeviceIdType.MESH
 
 
-VIA_X = ()
+VIA_X = {(0, False): (), (0, True): (), (1, False): (1,), (1, True): ()}
 PLANS = {
     (0, False): (
         "SW", "Z1", "R0", "R1", "Z2", "R2", "Z3", "SO", "SC", "W0", "OWN", "W1",
@@ -38,8 +38,8 @@
     (1, False): (
         "R0", "SW", "Z1", "R1", "R2", "Z2", "SO", "SC", "W0", "W1", "A0", "W2",
         "A1", "B0", "OWN", "W3", "A2", "B1", "W4", "A3", "B2", "XZ", "W5", "A4",
-        "B3", "A5", "B4", "P1", "B5", "P2", "WC", "OB", "Z3", "KE", "X1", "X2",
-        "RN", "ON", "Y1", "KV", "P3", "KX", "X3", "AT", "D1", "DZ", "Y2", "D2",
+        "B3", "A5", "B4", "P1", "B5", "P2", "WC", "OB", "Z3", "KE", "Y1", "X2",
+        "RN", "P3", "ON", "X1", "KV", "X3", "KX", "AT", "D1", "DZ", "Y2", "D2",
         "Y3", "D3",
     ),
     (1, True): (
@@ -72,7 +72,7 @@
     lengths, tokens, wq_hbm, wkv_hbm, cache_hbm, oproj_hbm,
     ig_hbm, pg_hbm, qgain, kgain, freq,
     out_ref,
-    igs, pgs, igain, pgain, cos_t, sin_t, xbuf, nbuf, w, cbuf, og, q_all, kv_all, q_snd, kv_snd, hsnd, ho, proj, obuf,
+    igs, pgs, igain, pgain, cos_t, sin_t, xbuf, nbuf, w, cbuf, og, q_all, kv_all, q_snd, kv_snd, hsnd, ho, proj, inv_s, obuf,
     lsem, osem, s_w, s_x, s_c, s_o, s_oz, s_kvx, s_kv, s_q, s_h,
     r_x, r_c, r_own, r_w, r_wc, r_o, r_oc, r_q, r_kv, r_kvx, r_h,
 ):
@@ -450,7 +450,7 @@
         "KX": wait_kvx, "AT": attention, "XZ": lambda: from_x(z), "DZ": lambda: from_diag(z),
     }
 
-    def step(tok):
+    def step(tok, via=()):
         if tok in ops:
             return ops[tok]()
         kind, k = tok[0], int(tok[1])
@@ -461,7 +461,7 @@
             if k < RC:
                 send_rows(k)
         else:
-            via_x = k in VIA_X
+            via_x = k in via
             for d in dist(k):
                 if kind == "Z":
                     z_to(d)
@@ -478,7 +478,7 @@
     plans = [PLANS[k] for k in kinds]
     first = 0
     while all(len(q) > first and q[first] == plans[0][first] for q in plans):
-        step(plans[0][first])
+        step(plans[0][first], VIA_X[kinds[0]])
         first += 1
     last = 0
     while all(len(q) > first + last and q[-1 - last] == plans[0][-1 - last] for q in plans):
@@ -488,9 +488,9 @@
             @pl.when((par == kp) & (mid == km))
             def _():
                 for tok in q[first : len(q) - last]:
-                    step(tok)
+                    step(tok, VIA_X[kp, km])
     for tok in plans[0][len(plans[0]) - last :]:
-        step(tok)
+        step(tok, VIA_X[kinds[0]])
     CC = chunk_of(DC, 1024)
     lo, hi = jnp.minimum(z, pt), jnp.maximum(z, pt)
     rest = []
@@ -498,7 +498,8 @@
         n = j + jnp.where(j >= lo, 1, 0)
         rest.append(n + jnp.where(n >= hi, 1, 0))
 
-    def project_out(pair, more):
+    def project_out(pair, more, last=False):
+        total = jnp.zeros((R, 128), F32)
         hv = jnp.concatenate([ho[n] for n in pair], axis=1)
         for k in range(S):
             def cols(i, carry):
@@ -508,10 +509,16 @@
                     [og[slab(k, kt, n), :, cs] for n in pair for kt in range(T)], axis=0
                 )
                 v = jnp.dot(hv, wt, preferred_element_type=F32)
-                proj[:, at] = proj[:, at] + v if more else v
+                if more:
+                    v = proj[:, at] + v
+                proj[:, at] = v
+                if last:
+                    for j in range(0, CC, 128):
+                        carry = carry + v[:, j : j + 128] * v[:, j : j + 128]
                 return carry
 
-            lax.fori_loop(0, DC // CC, cols, 0)
+            total = lax.fori_loop(0, DC // CC, cols, total)
+        return total
 
     X, Y = S - 1, T // 2 - 1
     near = (X + S) * (T // 2)
@@ -522,14 +529,16 @@
     for n in rest:
         arrived(ho.at[n], r_h.at[n])
     for j in range(0, N - 2, 2):
-        project_out(rest[j : j + 2], True)
+        total = project_out(rest[j : j + 2], True, j + 2 >= N - 2)
+    mean = jnp.sum(total, axis=1, keepdims=True) * (1.0 / D)
+    inv_s[...] = jnp.broadcast_to(lax.rsqrt(mean + EPSILON), (R, 128))
 
     RF = 16 if R % 16 == 0 else 8
 
     def finish(i, carry):
         rows = pl.ds(pl.multiple_of(i * RF, RF), RF)
         v = proj[rows, :]
-        inv = lax.rsqrt(jnp.sum(v * v, axis=1, keepdims=True) * (1.0 / D) + EPSILON)
+        inv = inv_s[rows, :][:, :1]
         obuf[rows, :] = (xbuf[b, rows, :].astype(F32) + v * inv * pgain[...]).astype(BF16)
         pltpu.make_async_copy(obuf.at[rows], out_ref.at[rows], osem).start()
         return carry
@@ -595,6 +604,7 @@
             pltpu.VMEM((N, R, HW), BF16),
             pltpu.VMEM((N, R, HW), BF16),
             pltpu.VMEM((R, D), F32),
+            pltpu.VMEM((R, 128), F32),
             pltpu.VMEM((R, D), BF16),
             dma((7,)), dma, dma, dma, dma, dma, dma, dma, dma, dma, dma,
             dma((h, RC)), dma((S,)), dma((NC,)), dma((T // 2, S2, NC)), dma, dma((S * T // 2 * N,)), dma((2,)),

time: 73.2 us -> 71.5 us (0.977)
  Pallas kernels: 70.8 us -> 69.1 us
    pallas_call x1, Pallas kernels: 70.8 us -> 69.1 us  [shards(): pl.pallas_call(functools.partial(kernel, T, S, N, S2, NC, RC), out_shape=...]
where the time goes in v4:
time: 71.5 us; the launch traced here: 71.4 us
  Pallas kernels  69.1 us (97%)
  local copies, waits for them, and re-layouts  2.25 us (3%)
    pallas_call x1, Pallas kernels, shards(): pl.pallas_call(functools.partial(kernel, T, S, N, S2, NC, RC), out_shape=...  69.1 us
    unnamed x1, local copies, waits for them, and re-layouts  2.25 us

profile of v4, /device:TPU:0, one launch (start us, length us, event | category | flops | bytes accessed | tf_op | source)
XLA Modules:
  0.0 71.4 jit_solution(12403668140063726654)
XLA Ops:
  0.0 69.1 %shard_map.109 = bf16[96,5376]{1,0:T(8,128)(2,1)} custom-call(s32[2]{0:T(128)} %lengths.1, bf16[96,5376]{1,0:T(8,128)(2,1)} %tokens.1, bf16[5376,128]{1,0:T(8,128)(2,1)} %wq_hbm.1, bf16[5376,256]{1,0:T(8,128)(2,1)} %wkv_hbm.1, bf16[512,256]{1,0:T(8,128)(2,1)} %cache_hbm.1, bf16[128,2688]{1,0:T(8,128)(2,1)} %oproj_hbm.1, f32[42,128]{1,0:T(8,128)} %bitcast.4, ...), custom_call_target="tpu_custom_call" | custom-call | tf_op jit(solution)/shard_map/pallas_call | solution.py:582
  69.1 2.2 %copy.13 = bf16[96,5376]{1,0:T(8,128)(2,1)} copy(bf16[96,5376]{1,0:T(8,128)(2,1)} %shard_map.109) | data formatting | bytes 2064384

commit v5 on v4

--- a/solution.py
+++ b/solution.py
@@ -491,7 +491,7 @@
                     step(tok, VIA_X[kp, km])
     for tok in plans[0][len(plans[0]) - last :]:
         step(tok, VIA_X[kinds[0]])
-    CC = chunk_of(DC, 1024)
+    CC = chunk_of(DC, 2048)
     lo, hi = jnp.minimum(z, pt), jnp.maximum(z, pt)
     rest = []
     for j in range(N - 2):
@@ -543,7 +543,7 @@
         pltpu.make_async_copy(obuf.at[rows], out_ref.at[rows], osem).start()
         return carry
 
-    lax.fori_loop(0, R // RF, finish, 0)
+    lax.fori_loop(0, R // RF, finish, 0, unroll=True)
 
     pltpu.make_async_copy(obuf, out_ref, osem).wait()
     left(w.at[1], s_w)

time: 71.5 us -> 71.2 us (level)
  no operation moved by 1% of the time
where the time goes in v5:
time: 71.2 us; the launch traced here: 71.1 us
  Pallas kernels  68.8 us (97%)
  local copies, waits for them, and re-layouts  2.25 us (3%)
    pallas_call x1, Pallas kernels, shards(): pl.pallas_call(functools.partial(kernel, T, S, N, S2, NC, RC), out_shape=...  68.8 us
    unnamed x1, local copies, waits for them, and re-layouts  2.25 us

profile of v5, /device:TPU:0, one launch (start us, length us, event | category | flops | bytes accessed | tf_op | source)
XLA Modules:
  0.0 71.1 jit_solution(10220033712233614483)
XLA Ops:
  0.0 68.8 %shard_map.109 = bf16[96,5376]{1,0:T(8,128)(2,1)} custom-call(s32[2]{0:T(128)} %lengths.1, bf16[96,5376]{1,0:T(8,128)(2,1)} %tokens.1, bf16[5376,128]{1,0:T(8,128)(2,1)} %wq_hbm.1, bf16[5376,256]{1,0:T(8,128)(2,1)} %wkv_hbm.1, bf16[512,256]{1,0:T(8,128)(2,1)} %cache_hbm.1, bf16[128,2688]{1,0:T(8,128)(2,1)} %oproj_hbm.1, f32[42,128]{1,0:T(8,128)} %bitcast.4, ...), custom_call_target="tpu_custom_call" | custom-call | tf_op jit(solution)/shard_map/pallas_call | solution.py:582
  68.8 2.2 %copy.13 = bf16[96,5376]{1,0:T(8,128)(2,1)} copy(bf16[96,5376]{1,0:T(8,128)(2,1)} %shard_map.109) | data formatting | bytes 2064384
